TPU v7x, 128 devices: a whole 4x4x4 slice. The times are simulated.
128 devices in a mesh: gx: 8 (over x, core), gy: 16 (over y, z).
Axes of the slice: x: 4, y: 4, z: 4, core: 2. Of those that a mesh axis runs over, the one named last changes fastest.
Arguments:
- feats: bfloat16 [524288, 192], P(('gx', 'gy')), may hold values from -6 to 6
- conv_weight: bfloat16 [27, 192, 192], replicated, may hold values from -0.125 to 0.125
- tap_index: int32 [524288, 27], P(('gx', 'gy')), may hold values from -1 to 8191, as said below
- halo_rows: int32 [128, 8, 512], P(('gx', 'gy')), may hold values from -1 to 4095, as said below
- hilbert_pos: int32 [524288], P(('gx', 'gy')), may hold values from 0 to 524287, as said below
- ln1_gain: float32 [192], replicated, may hold values from 0.1 to 1.9
- qkv_weight: bfloat16 [192, 576], replicated
- out_weight: bfloat16 [192, 192], replicated, may hold values from -0.4375 to 0.4375
- ln2_gain: float32 [192], replicated, may hold values from 0.1 to 1.9
- mlp_in: bfloat16 [192, 768], replicated, may hold values from -0.4375 to 0.4375
- mlp_out: bfloat16 [768, 192], replicated, may hold values from -0.21875 to 0.21875
Outputs:
- result: bfloat16 [524288, 192], P(('gx', 'gy'))
Inputs may be any that keep to these rules, and one draw needn't show every extreme that they name: `tap_index`: tap 13 of each point is the point's own row; below 4096: a row of the device's own points; 4096 + k * 512 + j: slot j of incoming list k. Within each aligned block of 128 points of a device and for each offset, all entries other than -1 lie in one aligned group of 128 rows of the lookup table (rows 128 g to 128 g + 127). `halo_rows`: -1 marks an empty slot; live slots of a list come first; every device has one list with all 512 slots live. `hilbert_pos`: A permutation of all points; device d's Hilbert range is positions d * 4096 to (d + 1) * 4096 - 1, with devices numbered x * 16 + y. Each point falls in the range of its own device or of a device whose x and y differ from its own by at most 1; at most 256 points of one device fall in one other device's range, exactly 256 for some pair in every draw.
All inputs are finite; a program needn't handle non-finite values.
Results may differ from a plain program's by a relative error of at most 0.0096.
Values may be sent and summed in bfloat16 or wider, within the bound.
A program may use at most 128 MiB of HBM per device.

v0:
```python
import math

import jax
import jax.numpy as jnp
from jax import lax
from jax.sharding import PartitionSpec as P

HEADS = 8
WIN = 1024


OFFSETS = ((-1, -1), (-1, 0), (-1, 1), (0, -1), (0, 1), (1, -1), (1, 0), (1, 1))


def with_halo(block, sides, width):
    for axis, dim in sides:
        count = lax.axis_size(axis)
        forward = [(i, i + 1) for i in range(count - 1)]
        backward = [(target, source) for source, target in forward]
        low = lax.ppermute(
            lax.slice_in_dim(block, block.shape[dim] - width, None, axis=dim), axis, forward
        )
        high = lax.ppermute(lax.slice_in_dim(block, 0, width, axis=dim), axis, backward)
        block = jnp.concatenate([low, block, high], axis=dim)
    return block


def layer_norm(values, gain):
    widened = values.astype(jnp.float32)
    average = jnp.mean(widened, -1, keepdims=True)
    centred = widened - average
    variance = jnp.mean(centred * centred, -1, keepdims=True)
    return (centred * lax.rsqrt(variance + 1e-05) * gain).astype(jnp.bfloat16)


def window_block(window, ln1_gain, qkv_weight, out_weight, ln2_gain, mlp_in, mlp_out):
    row_count, channels = window.shape
    head_dim = channels // HEADS
    normed = layer_norm(window, ln1_gain)
    packed = jnp.dot(normed, qkv_weight, preferred_element_type=jnp.float32).astype(jnp.bfloat16)
    queries = packed[:, :channels].reshape(row_count, HEADS, head_dim).transpose(1, 0, 2)
    key_rows = (
        packed[:, channels : 2 * channels].reshape(row_count, HEADS, head_dim).transpose(1, 0, 2)
    )
    values = packed[:, 2 * channels :].reshape(row_count, HEADS, head_dim).transpose(1, 0, 2)
    scaling = 1.0 / math.sqrt(head_dim)

    def one_head(triple):
        query_head, key_head, value_head = triple
        scores = jnp.dot(query_head, key_head.T, preferred_element_type=jnp.float32) * scaling
        weights = jax.nn.softmax(scores, axis=-1).astype(jnp.bfloat16)
        return jnp.dot(weights, value_head, preferred_element_type=jnp.float32).astype(jnp.bfloat16)

    attended = (
        lax.map(one_head, (queries, key_rows, values))
        .transpose(1, 0, 2)
        .reshape(row_count, channels)
    )
    residual = (
        window.astype(jnp.float32)
        + jnp.dot(attended, out_weight, preferred_element_type=jnp.float32)
    ).astype(jnp.bfloat16)
    normed_two = layer_norm(residual, ln2_gain)
    hidden = jax.nn.gelu(
        jnp.dot(normed_two, mlp_in, preferred_element_type=jnp.float32), approximate=False
    ).astype(jnp.bfloat16)
    return (
        residual.astype(jnp.float32) + jnp.dot(hidden, mlp_out, preferred_element_type=jnp.float32)
    ).astype(jnp.bfloat16)


def pick_incoming(padded):
    return jnp.stack([padded[2 + 2 * step_x, 2 + 2 * step_y] for step_x, step_y in OFFSETS])


def on_device(
    feats,
    conv_weight,
    tap_index,
    halo_rows,
    hilbert_pos,
    ln1_gain,
    qkv_weight,
    out_weight,
    ln2_gain,
    mlp_in,
    mlp_out,
):
    points, channels = feats.shape
    lists = halo_rows[0]
    halo_depth = lists.shape[1]
    picked = feats[jnp.maximum(lists, 0)]
    outgoing = jnp.where((lists >= 0)[:, :, None], picked, jnp.zeros_like(picked))
    centre = jnp.zeros((1, halo_depth, channels), feats.dtype)
    faces_grid = jnp.concatenate([outgoing[:4], centre, outgoing[4:]], 0).reshape(
        3, 3, halo_depth, channels
    )
    padded = with_halo(faces_grid, (("gx", 0), ("gy", 1)), 1)
    incoming = pick_incoming(padded)
    lookup = jnp.concatenate([feats, incoming.reshape(8 * halo_depth, channels)], 0)
    group_table = lookup.reshape(-1, 128, channels)
    tap_count = tap_index.shape[1]
    tile_total = points // 128
    tile_step = min(4, tile_total)
    tile_taps = tap_index.reshape(tile_total, 128, tap_count)
    tile_groups = jnp.maximum(jnp.max(tile_taps, 1), 0) // 128
    flat_weight = conv_weight.reshape(-1, channels)
    columns = jnp.arange(128, dtype=jnp.int32)

    def conv_block(pair):
        block_taps, block_groups = pair
        within = block_taps - block_groups[:, None, :] * 128
        sources = group_table[block_groups]
        onehot = (within[..., None] == columns).astype(jnp.bfloat16)
        taken = jnp.einsum(
            "irtk,itkc->irtc", onehot, sources, preferred_element_type=jnp.float32
        ).astype(jnp.bfloat16)
        return jnp.dot(
            taken.reshape(tile_step * 128, tap_count * channels),
            flat_weight,
            preferred_element_type=jnp.float32,
        )

    conv_out = lax.map(
        conv_block,
        (
            tile_taps.reshape(tile_total // tile_step, tile_step, 128, tap_count),
            tile_groups.reshape(tile_total // tile_step, tile_step, tap_count),
        ),
    ).reshape(points, channels)
    updated = (feats.astype(jnp.float32) + conv_out).astype(jnp.bfloat16)
    along_y = lax.axis_size("gy")
    index_x = lax.axis_index("gx")
    index_y = lax.axis_index("gy")
    capacity = points // 16
    target = hilbert_pos // points
    step_x = target // along_y - index_x
    step_y = target % along_y - index_y
    code = 3 * (step_x + 1) + (step_y + 1)
    onehot_code = (code[:, None] == jnp.arange(9, dtype=jnp.int32)[None, :]).astype(jnp.int32)
    before = jnp.sum((jnp.cumsum(onehot_code, 0) - onehot_code) * onehot_code, 1)
    local_spot = hilbert_pos - target * points
    sending = code != 4
    dump = 9 * capacity
    place = jnp.where(sending, code * capacity + before, dump)
    out_rows = (
        jnp.zeros((dump + 1, channels), jnp.bfloat16)
        .at[place]
        .set(updated)[:dump]
        .reshape(3, 3, capacity, channels)
    )
    out_spots = (
        jnp.zeros((dump + 1,), jnp.int32)
        .at[place]
        .set(local_spot + 1)[:dump]
        .reshape(3, 3, capacity)
    )
    rows_pad, spots_pad = (
        with_halo(out_rows, (("gx", 0), ("gy", 1)), 1),
        with_halo(out_spots, (("gx", 0), ("gy", 1)), 1),
    )
    in_rows = pick_incoming(rows_pad)
    in_spots = pick_incoming(spots_pad) - 1
    holder = jnp.where(in_spots < 0, points, in_spots).reshape(-1)
    own_holder = jnp.where(sending, points, local_spot)
    ordered = (
        jnp.zeros((points + 1, channels), jnp.bfloat16)
        .at[jnp.concatenate([own_holder, holder])]
        .set(jnp.concatenate([updated, in_rows.reshape(-1, channels)], 0))[:points]
    )
    windows = ordered.reshape(points // WIN, WIN, channels)
    processed = lax.map(
        lambda window: window_block(
            window, ln1_gain, qkv_weight, out_weight, ln2_gain, mlp_in, mlp_out
        ),
        windows,
    ).reshape(points, channels)
    returning = processed[jnp.maximum(in_spots, 0)]
    middle = jnp.zeros((1, capacity, channels), jnp.bfloat16)
    back_grid = jnp.concatenate([returning[:4], middle, returning[4:]], 0).reshape(
        3, 3, capacity, channels
    )
    back_pad = with_halo(back_grid, (("gx", 0), ("gy", 1)), 1)
    arrived = pick_incoming(back_pad).reshape(8 * capacity, channels)
    list_number = code - (code > 4).astype(jnp.int32)
    table = jnp.concatenate([processed, arrived], 0)
    fetch = jnp.where(sending, points + list_number * capacity + before, local_spot)
    return table[fetch]


def solution(mesh):
    placed = (
        P(("gx", "gy"), None),
        P(),
        P(("gx", "gy"), None),
        P(("gx", "gy"), None, None),
        P(("gx", "gy")),
        P(),
        P(),
        P(),
        P(),
        P(),
        P(),
    )
    return jax.shard_map(
        on_device, mesh=mesh, in_specs=placed, out_specs=P(("gx", "gy"), None), check_vma=False
    )
```

profile of v0, /device:TPU:25, one launch (start us, length us, event | category | flops | bytes accessed | tf_op | source)
XLA Modules:
  0.0 662.7 jit_solution(8378735180842922945)
XLA Ops:
  9.6 16.9 %gather_fusion.1 = bf16[4096,192]{1,0:T(8,128)(2,1)} fusion(bf16[4096,192]{1,0:T(8,128)(2,1)S(1)} %copy.221, s32[4096]{0:T(1024)S(1)} %get-tuple-element.360), kind=kCustom, calls=%fused_computation.1 | custom fusion | bytes 3162112 | tf_op jit(solution)/shard_map/gather | solution.py:92
  36.3 15.5 %scatter_custom_fusion = s32[2305]{0:T(1024)S(1)} fusion(s32[4096]{0:T(1024)S(1)} %get-tuple-element.348, s32[4096]{0:T(1024)S(1)} %get-tuple-element.351, s32[]{:T(128)} %constant.199.clone.1), kind=kCustom, calls=%fused_computation.248 | custom fusion | bytes 9224 | tf_op jit(solution)/shard_map/scatter | solution.py:155
  61.2 5.8 collective-permute-start.3
  77.6 6.0 collective-permute-start.7
  84.2 19.1 %collective-permute-done.6 = bf16[5,1,512,192]{2,3,1,0:T(8,128)(2,1)S(1)} collective-permute-done((bf16[5,1,512,192]{2,3,1,0:T(8,128)(2,1)S(1)}, bf16[5,1,512,192]{2,3,1,0:T(8,128)(2,1)S(1)}, u32[]{:S(2)}, u32[]{:S(2)}) %collective-permute-start.6) | collective-permute-done | bytes 983072 | tf_op jit(solution)/shard_map/ppermute | solution.py:20
  107.5 5.9 copy.246
  113.5 259.3 %while.33 = (s32[]{:T(128)}, f32[8,512,192]{1,0,2:T(8,128)}, s32[8,4,27]{2,1,0:T(4,128)S(1)}, bf16[64,128,192]{2,1,0:T(8,128)(2,1)}, s32[8,4,128,27]{2,1,0,3:T(4...) while((s32[]{:T(128)}, f32[8,512,192]{1,0,2:T(8,128)}, ...), condition=%wide.region_6.7_spmd.clone, body=%wide.region_5.6_spmd.clone.sunk | while | flops 1703132160 | bytes 41400212 | solution.py:124
  113.7 8.4 %gather_fusion = bf16[108,128,192]{2,1,0:T(8,128)(2,1)} fusion(bf16[64,128,192]{2,1,0:T(8,128)(2,1)} %get-tuple-element.548, s32[1024]{0:T(1024)S(1)} %pad_clamp_fusion.2), kind=kCustom, calls=%fused_computation.clone.clone.1 | custom fusion | bytes 10617264 | tf_op jit(solution)/shard_map/while/body/eval_jaxpr/gather | solution.py:113
  122.1 6.5 convert_bitcast_fusion.3
  137.0 8.9 %dynamic_update_slice.19 = f32[8,512,192]{1,0,2:T(8,128)} dynamic-update-slice(f32[8,512,192]{1,0,2:T(8,128)} %get-tuple-element.538, f32[1,512,192]{1,0,2:T(1,128)S(1)} %copy.284, s32[]{:T(128)} %get-tuple-element.537, s32[]{:T(128)} %constant.199.clone.1..sunk.1, s32[]{:T(128)} %constant.199.clone.1..sunk.1) | dynamic-update-slice | bytes 786436 | tf_op jit(solution)/shard_map/while/body/jit(dynamic_update_index_in_dim)/dynamic_update_slice | solution.py:124
  146.1 8.4 %gather_fusion = bf16[108,128,192]{2,1,0:T(8,128)(2,1)} fusion(bf16[64,128,192]{2,1,0:T(8,128)(2,1)} %get-tuple-element.548, s32[1024]{0:T(1024)S(1)} %pad_clamp_fusion.2), kind=kCustom, calls=%fused_computation.clone.clone.1 | custom fusion | bytes 10617264 | tf_op jit(solution)/shard_map/while/body/eval_jaxpr/gather | solution.py:113
  154.5 6.5 convert_bitcast_fusion.3
  169.4 8.9 %dynamic_update_slice.19 = f32[8,512,192]{1,0,2:T(8,128)} dynamic-update-slice(f32[8,512,192]{1,0,2:T(8,128)} %get-tuple-element.538, f32[1,512,192]{1,0,2:T(1,128)S(1)} %copy.284, s32[]{:T(128)} %get-tuple-element.537, s32[]{:T(128)} %constant.199.clone.1..sunk.1, s32[]{:T(128)} %constant.199.clone.1..sunk.1) | dynamic-update-slice | bytes 786436 | tf_op jit(solution)/shard_map/while/body/jit(dynamic_update_index_in_dim)/dynamic_update_slice | solution.py:124
  178.5 8.4 %gather_fusion = bf16[108,128,192]{2,1,0:T(8,128)(2,1)} fusion(bf16[64,128,192]{2,1,0:T(8,128)(2,1)} %get-tuple-element.548, s32[1024]{0:T(1024)S(1)} %pad_clamp_fusion.2), kind=kCustom, calls=%fused_computation.clone.clone.1 | custom fusion | bytes 10617264 | tf_op jit(solution)/shard_map/while/body/eval_jaxpr/gather | solution.py:113
  186.9 6.5 convert_bitcast_fusion.3
  201.8 8.9 %dynamic_update_slice.19 = f32[8,512,192]{1,0,2:T(8,128)} dynamic-update-slice(f32[8,512,192]{1,0,2:T(8,128)} %get-tuple-element.538, f32[1,512,192]{1,0,2:T(1,128)S(1)} %copy.284, s32[]{:T(128)} %get-tuple-element.537, s32[]{:T(128)} %constant.199.clone.1..sunk.1, s32[]{:T(128)} %constant.199.clone.1..sunk.1) | dynamic-update-slice | bytes 786436 | tf_op jit(solution)/shard_map/while/body/jit(dynamic_update_index_in_dim)/dynamic_update_slice | solution.py:124
  210.9 8.4 %gather_fusion = bf16[108,128,192]{2,1,0:T(8,128)(2,1)} fusion(bf16[64,128,192]{2,1,0:T(8,128)(2,1)} %get-tuple-element.548, s32[1024]{0:T(1024)S(1)} %pad_clamp_fusion.2), kind=kCustom, calls=%fused_computation.clone.clone.1 | custom fusion | bytes 10617264 | tf_op jit(solution)/shard_map/while/body/eval_jaxpr/gather | solution.py:113
  219.3 6.5 convert_bitcast_fusion.3
  234.2 8.9 %dynamic_update_slice.19 = f32[8,512,192]{1,0,2:T(8,128)} dynamic-update-slice(f32[8,512,192]{1,0,2:T(8,128)} %get-tuple-element.538, f32[1,512,192]{1,0,2:T(1,128)S(1)} %copy.284, s32[]{:T(128)} %get-tuple-element.537, s32[]{:T(128)} %constant.199.clone.1..sunk.1, s32[]{:T(128)} %constant.199.clone.1..sunk.1) | dynamic-update-slice | bytes 786436 | tf_op jit(solution)/shard_map/while/body/jit(dynamic_update_index_in_dim)/dynamic_update_slice | solution.py:124
  243.3 8.4 %gather_fusion = bf16[108,128,192]{2,1,0:T(8,128)(2,1)} fusion(bf16[64,128,192]{2,1,0:T(8,128)(2,1)} %get-tuple-element.548, s32[1024]{0:T(1024)S(1)} %pad_clamp_fusion.2), kind=kCustom, calls=%fused_computation.clone.clone.1 | custom fusion | bytes 10617264 | tf_op jit(solution)/shard_map/while/body/eval_jaxpr/gather | solution.py:113
  251.7 6.5 convert_bitcast_fusion.3
  266.6 8.9 %dynamic_update_slice.19 = f32[8,512,192]{1,0,2:T(8,128)} dynamic-update-slice(f32[8,512,192]{1,0,2:T(8,128)} %get-tuple-element.538, f32[1,512,192]{1,0,2:T(1,128)S(1)} %copy.284, s32[]{:T(128)} %get-tuple-element.537, s32[]{:T(128)} %constant.199.clone.1..sunk.1, s32[]{:T(128)} %constant.199.clone.1..sunk.1) | dynamic-update-slice | bytes 786436 | tf_op jit(solution)/shard_map/while/body/jit(dynamic_update_index_in_dim)/dynamic_update_slice | solution.py:124
  275.7 8.4 %gather_fusion = bf16[108,128,192]{2,1,0:T(8,128)(2,1)} fusion(bf16[64,128,192]{2,1,0:T(8,128)(2,1)} %get-tuple-element.548, s32[1024]{0:T(1024)S(1)} %pad_clamp_fusion.2), kind=kCustom, calls=%fused_computation.clone.clone.1 | custom fusion | bytes 10617264 | tf_op jit(solution)/shard_map/while/body/eval_jaxpr/gather | solution.py:113
  284.1 6.5 convert_bitcast_fusion.3
  299.0 8.9 %dynamic_update_slice.19 = f32[8,512,192]{1,0,2:T(8,128)} dynamic-update-slice(f32[8,512,192]{1,0,2:T(8,128)} %get-tuple-element.538, f32[1,512,192]{1,0,2:T(1,128)S(1)} %copy.284, s32[]{:T(128)} %get-tuple-element.537, s32[]{:T(128)} %constant.199.clone.1..sunk.1, s32[]{:T(128)} %constant.199.clone.1..sunk.1) | dynamic-update-slice | bytes 786436 | tf_op jit(solution)/shard_map/while/body/jit(dynamic_update_index_in_dim)/dynamic_update_slice | solution.py:124
  308.1 8.4 %gather_fusion = bf16[108,128,192]{2,1,0:T(8,128)(2,1)} fusion(bf16[64,128,192]{2,1,0:T(8,128)(2,1)} %get-tuple-element.548, s32[1024]{0:T(1024)S(1)} %pad_clamp_fusion.2), kind=kCustom, calls=%fused_computation.clone.clone.1 | custom fusion | bytes 10617264 | tf_op jit(solution)/shard_map/while/body/eval_jaxpr/gather | solution.py:113
  316.5 6.5 convert_bitcast_fusion.3
  331.4 8.9 %dynamic_update_slice.19 = f32[8,512,192]{1,0,2:T(8,128)} dynamic-update-slice(f32[8,512,192]{1,0,2:T(8,128)} %get-tuple-element.538, f32[1,512,192]{1,0,2:T(1,128)S(1)} %copy.284, s32[]{:T(128)} %get-tuple-element.537, s32[]{:T(128)} %constant.199.clone.1..sunk.1, s32[]{:T(128)} %constant.199.clone.1..sunk.1) | dynamic-update-slice | bytes 786436 | tf_op jit(solution)/shard_map/while/body/jit(dynamic_update_index_in_dim)/dynamic_update_slice | solution.py:124
  340.5 8.4 %gather_fusion = bf16[108,128,192]{2,1,0:T(8,128)(2,1)} fusion(bf16[64,128,192]{2,1,0:T(8,128)(2,1)} %get-tuple-element.548, s32[1024]{0:T(1024)S(1)} %pad_clamp_fusion.2), kind=kCustom, calls=%fused_computation.clone.clone.1 | custom fusion | bytes 10617264 | tf_op jit(solution)/shard_map/while/body/eval_jaxpr/gather | solution.py:113
  348.9 6.5 convert_bitcast_fusion.3
  363.8 8.9 %dynamic_update_slice.19 = f32[8,512,192]{1,0,2:T(8,128)} dynamic-update-slice(f32[8,512,192]{1,0,2:T(8,128)} %get-tuple-element.538, f32[1,512,192]{1,0,2:T(1,128)S(1)} %copy.284, s32[]{:T(128)} %get-tuple-element.537, s32[]{:T(128)} %constant.199.clone.1..sunk.1, s32[]{:T(128)} %constant.199.clone.1..sunk.1) | dynamic-update-slice | bytes 786436 | tf_op jit(solution)/shard_map/while/body/jit(dynamic_update_index_in_dim)/dynamic_update_slice | solution.py:124
  380.3 18.5 %scatter_custom_fusion.1 = bf16[2305,192]{1,0:T(8,128)(2,1)S(1)} fusion(s32[4096]{0:T(1024)S(1)} %get-tuple-element.348, bf16[4096,192]{1,0:T(8,128)(2,1)} %copy.227, bf16[]{:T(256)} %constant.200.clone.1), kind=kCustom, calls=%fused_computation.133 | custom fusion | bytes 885632 | tf_op jit(solution)/shard_map/scatter | solution.py:149
  422.1 6.2 collective-permute-start.11
  442.6 27.3 %scatter_custom_fusion.2 = bf16[4097,192]{1,0:T(8,128)(2,1)S(1)} fusion(s32[6144]{0:T(1024)} %bitcast.361, bf16[6144,192]{1,0:T(8,128)(2,1)} %copy.236, bf16[]{:T(256)} %constant.200.clone.1), kind=kCustom, calls=%fused_computation.128 | custom fusion | bytes 1573760 | tf_op jit(solution)/shard_map/scatter | solution.py:169
  474.6 119.4 %while.32 = (s32[]{:T(128)}, bf16[4,1024,192]{1,2,0:T(8,128)(2,1)}, bf16[4,1024,192]{1,2,0:T(8,128)(2,1)S(1)}, f32[192]{0:T(256)S(1)}, bf16[192,576]{1,0:T(8,128...) while((s32[]{:T(128)}, bf16[4,1024,192]{1,2,0:T(8,128)(2,1)}, ...), condition=%wide.region_18.19_spmd, body=%wide.region_9.18_spmd.sunk | while | flops 1072717824 | bytes 22831872 | solution.py:172
  475.6 19.0 %while.34 = (s32[]{:T(128)}, bf16[8,1024,24]{1,2,0:T(8,128)(2,1)S(1)}, bf16[8,1024,24]{1,2,0:T(8,128)(2,1)S(1)}, bf16[8,1024,24]{1,2,0:T(8,128)(2,1)S(1)}, bf16[8,1024,24]{1,2,0:T(8,128)(2,1)S(1)}, /*index=5*/s32[]{:T(128)}) while((s32[]{:T(128)}, bf16[8,1024,24]{1,2,0:T(8,128)(2,1)S(1)}, bf16[8,1024,24]{1,2,0:T(8,128)(2,1)S(1)}, ...), condition=%wide.region_15.15_spmd, body=%wide.region_12.14_spmd.sunk | while | flops 110123008 | bytes 12802117 | solution.py:55
  495.0 9.5 %fusion.180 = bf16[4,1024,192]{1,2,0:T(8,128)(2,1)} fusion(bf16[4,1024,192]{1,2,0:T(8,128)(2,1)} %get-tuple-element.566, s32[]{:T(128)} %get-tuple-element.565, f32[1024,192]{0,1:T(8,128)S(1)} %get-tuple-element.495, bf16[768,192]{0,1:T(8,128)(2,1)} %get-tuple-element.585, bf16[192,768]{1,0:T(8,128)(2,1)} %get-tuple-element.584, ...), kind=kOutput, calls=%fused_computation.53.clone.1 | convolution fusion | flops 656277504 | bytes 2565632 | tf_op jit(solution)/shard_map/while/body/eval_jaxpr/dot_general | solution.py:68
  505.4 19.0 %while.34 = (s32[]{:T(128)}, bf16[8,1024,24]{1,2,0:T(8,128)(2,1)S(1)}, bf16[8,1024,24]{1,2,0:T(8,128)(2,1)S(1)}, bf16[8,1024,24]{1,2,0:T(8,128)(2,1)S(1)}, bf16[8,1024,24]{1,2,0:T(8,128)(2,1)S(1)}, /*index=5*/s32[]{:T(128)}) while((s32[]{:T(128)}, bf16[8,1024,24]{1,2,0:T(8,128)(2,1)S(1)}, bf16[8,1024,24]{1,2,0:T(8,128)(2,1)S(1)}, ...), condition=%wide.region_15.15_spmd, body=%wide.region_12.14_spmd.sunk | while | flops 110123008 | bytes 12802117 | solution.py:55
  524.9 9.5 %fusion.180 = bf16[4,1024,192]{1,2,0:T(8,128)(2,1)} fusion(bf16[4,1024,192]{1,2,0:T(8,128)(2,1)} %get-tuple-element.566, s32[]{:T(128)} %get-tuple-element.565, f32[1024,192]{0,1:T(8,128)S(1)} %get-tuple-element.495, bf16[768,192]{0,1:T(8,128)(2,1)} %get-tuple-element.585, bf16[192,768]{1,0:T(8,128)(2,1)} %get-tuple-element.584, ...), kind=kOutput, calls=%fused_computation.53.clone.1 | convolution fusion | flops 656277504 | bytes 2565632 | tf_op jit(solution)/shard_map/while/body/eval_jaxpr/dot_general | solution.py:68
  535.2 19.0 %while.34 = (s32[]{:T(128)}, bf16[8,1024,24]{1,2,0:T(8,128)(2,1)S(1)}, bf16[8,1024,24]{1,2,0:T(8,128)(2,1)S(1)}, bf16[8,1024,24]{1,2,0:T(8,128)(2,1)S(1)}, bf16[8,1024,24]{1,2,0:T(8,128)(2,1)S(1)}, /*index=5*/s32[]{:T(128)}) while((s32[]{:T(128)}, bf16[8,1024,24]{1,2,0:T(8,128)(2,1)S(1)}, bf16[8,1024,24]{1,2,0:T(8,128)(2,1)S(1)}, ...), condition=%wide.region_15.15_spmd, body=%wide.region_12.14_spmd.sunk | while | flops 110123008 | bytes 12802117 | solution.py:55
  554.7 9.5 %fusion.180 = bf16[4,1024,192]{1,2,0:T(8,128)(2,1)} fusion(bf16[4,1024,192]{1,2,0:T(8,128)(2,1)} %get-tuple-element.566, s32[]{:T(128)} %get-tuple-element.565, f32[1024,192]{0,1:T(8,128)S(1)} %get-tuple-element.495, bf16[768,192]{0,1:T(8,128)(2,1)} %get-tuple-element.585, bf16[192,768]{1,0:T(8,128)(2,1)} %get-tuple-element.584, ...), kind=kOutput, calls=%fused_computation.53.clone.1 | convolution fusion | flops 656277504 | bytes 2565632 | tf_op jit(solution)/shard_map/while/body/eval_jaxpr/dot_general | solution.py:68
  565.1 19.0 %while.34 = (s32[]{:T(128)}, bf16[8,1024,24]{1,2,0:T(8,128)(2,1)S(1)}, bf16[8,1024,24]{1,2,0:T(8,128)(2,1)S(1)}, bf16[8,1024,24]{1,2,0:T(8,128)(2,1)S(1)}, bf16[8,1024,24]{1,2,0:T(8,128)(2,1)S(1)}, /*index=5*/s32[]{:T(128)}) while((s32[]{:T(128)}, bf16[8,1024,24]{1,2,0:T(8,128)(2,1)S(1)}, bf16[8,1024,24]{1,2,0:T(8,128)(2,1)S(1)}, ...), condition=%wide.region_15.15_spmd, body=%wide.region_12.14_spmd.sunk | while | flops 110123008 | bytes 12802117 | solution.py:55
  584.5 9.5 %fusion.180 = bf16[4,1024,192]{1,2,0:T(8,128)(2,1)} fusion(bf16[4,1024,192]{1,2,0:T(8,128)(2,1)} %get-tuple-element.566, s32[]{:T(128)} %get-tuple-element.565, f32[1024,192]{0,1:T(8,128)S(1)} %get-tuple-element.495, bf16[768,192]{0,1:T(8,128)(2,1)} %get-tuple-element.585, bf16[192,768]{1,0:T(8,128)(2,1)} %get-tuple-element.584, ...), kind=kOutput, calls=%fused_computation.53.clone.1 | convolution fusion | flops 656277504 | bytes 2565632 | tf_op jit(solution)/shard_map/while/body/eval_jaxpr/dot_general | solution.py:68
  597.0 7.5 %gather_fusion.2 = bf16[2048,192]{1,0:T(8,128)(2,1)S(1)} fusion(bf16[4096,192]{1,0:T(8,128)(2,1)S(1)} %bitcast.324, s32[2048]{0:T(1024)S(1)} %copy-done.6), kind=kCustom, calls=%fused_computation.2 | custom fusion | bytes 1581056 | tf_op jit(solution)/shard_map/gather | solution.py:178
  607.2 5.3 collective-permute-start.12
  624.6 6.2 collective-permute-start.15
  630.8 5.2 collective-permute-done.14
  641.6 16.9 %gather_fusion.3 = bf16[4096,192]{1,0:T(8,128)(2,1)} fusion(bf16[6144,192]{1,0:T(8,128)(2,1)S(1)} %pad_maximum_fusion.1, s32[4096]{0:T(1024)S(1)} %copy-done.5), kind=kCustom, calls=%fused_computation.3 | custom fusion | bytes 3162112 | tf_op jit(solution)/shard_map/gather | solution.py:188
  (383 shorter events, 269.1 us)
Async XLA Ops:
  0.0 8.9 %copy-start.4 = (s32[4096]{0:T(1024)S(1)}, s32[4096]{0:T(1024)}, u32[]{:S(2)}) copy-start(s32[4096]{0:T(1024)} %param.21) | copy-start | bytes 49156
  30.7 43.5 %collective-permute-start.4 = (bf16[1,3,512,192]{2,3,1,0:T(8,128)(2,1)}, bf16[1,3,512,192]{2,3,1,0:T(8,128)(2,1)}, u32[]{:S(2)}, u32[]{:S(2)}) collective-permute-start(bf16[1,3,512,192]{2,3,1,0:T(8,128)(2,1)} %get-tuple-element.335), channel_id=1, source_target_pairs={{0,16},{16,32},{32,48},{48,64},{64,80},{80,96},{96,112},{1,17},{17... | collective-permute-start | bytes 1769480 | tf_op jit(solution)/shard_map/ppermute | solution.py:20
  34.4 39.8 %collective-permute-start.5 = (bf16[1,3,512,192]{2,3,1,0:T(8,128)(2,1)}, bf16[1,3,512,192]{2,3,1,0:T(8,128)(2,1)}, u32[]{:S(2)}, u32[]{:S(2)}) collective-permute-start(bf16[1,3,512,192]{2,3,1,0:T(8,128)(2,1)} %get-tuple-element.336), channel_id=1, source_target_pairs={{16,0},{32,16},{48,32},{64,48},{80,64},{96,80},{112,96},{17,1},{33... | collective-permute-start | bytes 1769480 | tf_op jit(solution)/shard_map/ppermute | solution.py:23
  51.8 9.3 %collective-permute-start = (s32[1,3,256]{2,1,0:T(4,128)S(1)}, s32[1,3,256]{2,1,0:T(4,128)S(1)}, u32[]{:S(2)}, u32[]{:S(2)}) collective-permute-start(s32[1,3,256]{2,1,0:T(4,128)S(1)} %slice.223), channel_id=1, source_target_pairs={{0,16},{16,32},{32,48},{48,64},{64,80},{80,96},{96,112},{1,17},{17... | collective-permute-start | bytes 9224 | tf_op jit(solution)/shard_map/ppermute | solution.py:20
  55.5 5.7 collective-permute-start.1
  59.5 1.6 copy-start.13
  61.2 43.2 %copy-start.10 = (s32[1,3,256]{2,1,0:T(4,128)}, s32[1,3,256]{2,1,0:T(4,128)S(1)}, u32[]{:S(2)}) copy-start(s32[1,3,256]{2,1,0:T(4,128)S(1)} %collective-permute-done.1) | copy-start | bytes 9220
  61.2 7.8 %collective-permute-start.3 = (s32[5,1,256]{2,1,0:T(1,128)S(1)}, s32[5,1,256]{2,1,0:T(1,128)S(1)}, u32[]{:S(2)}, u32[]{:S(2)}) collective-permute-start(s32[5,1,256]{2,1,0:T(1,128)S(1)} %get-tuple-element.349), channel_id=1, source_target_pairs={{1,0},{2,1},{3,2},{4,3},{5,4},{6,5},{7,6},{8,7},{9,8},{10,9},{11,1... | collective-permute-start | bytes 15368 | tf_op jit(solution)/shard_map/ppermute | solution.py:23
  67.1 6.5 collective-permute-start.2
  69.0 35.4 %copy-start.11 = (s32[5,1,256]{2,1,0:T(1,128)}, s32[5,1,256]{2,1,0:T(1,128)S(1)}, u32[]{:S(2)}) copy-start(s32[5,1,256]{2,1,0:T(1,128)S(1)} %collective-permute-done.3) | copy-start | bytes 15364
  73.6 0.6 copy-start.12
  75.6 27.7 %collective-permute-start.6 = (bf16[5,1,512,192]{2,3,1,0:T(8,128)(2,1)S(1)}, bf16[5,1,512,192]{2,3,1,0:T(8,128)(2,1)S(1)}, u32[]{:S(2)}, u32[]{:S(2)}) collective-permute-start(bf16[5,1,512,192]{2,3,1,0:T(8,128)(2,1)S(1)} %get-tuple-element.332), channel_id=1, source_target_pairs={{0,1},{1,2},{2,3},{3,4},{4,5},{5,6},{6,7},{7,8},{8,9},{9,10},{10,1... | collective-permute-start | bytes 2949128 | tf_op jit(solution)/shard_map/ppermute | solution.py:20
  77.6 28.0 %copy-start.8 = (s32[8,256,1]{1,2,0:T(1,128)}, s32[8,256,1]{1,2,0:T(1,128)S(1)}, u32[]{:S(2)}) copy-start(s32[8,256,1]{1,2,0:T(1,128)S(1)} %constant_dynamic-update-slice_fusion.6) | copy-start | bytes 24580
  77.6 26.7 %collective-permute-start.7 = (bf16[5,1,512,192]{2,3,1,0:T(8,128)(2,1)S(1)}, bf16[5,1,512,192]{2,3,1,0:T(8,128)(2,1)S(1)}, u32[]{:S(2)}, u32[]{:S(2)}) collective-permute-start(bf16[5,1,512,192]{2,3,1,0:T(8,128)(2,1)S(1)} %get-tuple-element.331), channel_id=1, source_target_pairs={{1,0},{2,1},{3,2},{4,3},{5,4},{6,5},{7,6},{8,7},{9,8},{10,9},{11,1... | collective-permute-start | bytes 2949128 | tf_op jit(solution)/shard_map/ppermute | solution.py:23
  84.2 21.4 %copy-start.1 = (bf16[4096,192]{0,1:T(8,128)(2,1)S(1)}, bf16[4096,192]{0,1:T(8,128)(2,1)}, u32[]{:S(2)}) copy-start(bf16[4096,192]{0,1:T(8,128)(2,1)} %param.17) | copy-start | bytes 4718596
  377.8 30.3 %copy-start.9 = (s32[8,256,1]{1,2,0:T(1,128)S(1)}, s32[8,256,1]{1,2,0:T(1,128)}, u32[]{:S(2)}) copy-start(s32[8,256,1]{1,2,0:T(1,128)} %copy-done.8) | copy-start | bytes 24580
  401.6 11.7 %collective-permute-start.8 = (bf16[1,3,256,192]{2,1,3,0:T(4,128)(2,1)}, bf16[1,3,256,192]{2,1,3,0:T(4,128)(2,1)}, u32[]{:S(2)}, u32[]{:S(2)}) collective-permute-start(bf16[1,3,256,192]{2,1,3,0:T(4,128)(2,1)} %copy.247), channel_id=1, source_target_pairs={{0,16},{16,32},{32,48},{48,64},{64,80},{80,96},{96,112},{1,17},{17... | collective-permute-start | bytes 884744 | tf_op jit(solution)/shard_map/ppermute | solution.py:20
  406.2 9.3 %collective-permute-start.9 = (bf16[1,3,256,192]{2,1,0,3:T(4,128)(2,1)}, bf16[1,3,256,192]{2,1,0,3:T(4,128)(2,1)S(1)}, u32[]{:S(2)}, u32[]{:S(2)}) collective-permute-start(bf16[1,3,256,192]{2,1,0,3:T(4,128)(2,1)} %copy.231), channel_id=1, source_target_pairs={{16,0},{32,16},{48,32},{64,48},{80,64},{96,80},{112,96},{17,1},{33... | collective-permute-start | bytes 884744 | tf_op jit(solution)/shard_map/ppermute | solution.py:23
  419.4 14.4 %collective-permute-start.10 = (bf16[5,1,256,192]{2,3,1,0:T(8,128)(2,1)S(1)}, bf16[5,1,256,192]{2,3,1,0:T(8,128)(2,1)S(1)}, u32[]{:S(2)}, u32[]{:S(2)}) collective-permute-start(bf16[5,1,256,192]{2,3,1,0:T(8,128)(2,1)S(1)} %copy.233), channel_id=1, source_target_pairs={{0,1},{1,2},{2,3},{3,4},{4,5},{5,6},{6,7},{7,8},{8,9},{9,10},{10,1... | collective-permute-start | bytes 1474568 | tf_op jit(solution)/shard_map/ppermute | solution.py:20
  422.1 14.2 %collective-permute-start.11 = (bf16[5,1,256,192]{2,3,1,0:T(8,128)(2,1)S(1)}, bf16[5,1,256,192]{2,3,1,0:T(8,128)(2,1)S(1)}, u32[]{:S(2)}, u32[]{:S(2)}) collective-permute-start(bf16[5,1,256,192]{2,3,1,0:T(8,128)(2,1)S(1)} %copy.234), channel_id=1, source_target_pairs={{1,0},{2,1},{3,2},{4,3},{5,4},{6,5},{7,6},{8,7},{9,8},{10,9},{11,1... | collective-permute-start | bytes 1474568 | tf_op jit(solution)/shard_map/ppermute | solution.py:23
  469.9 4.7 copy-start.2
  470.0 4.6 copy-start.3
  470.0 4.6 copy-start.7
  470.0 4.6 copy-start.15
  594.0 3.0 copy-start.6
  597.0 7.5 %copy-start = (bf16[4,1024,192]{2,1,0:T(8,128)(2,1)}, bf16[4,1024,192]{2,1,0:T(8,128)(2,1)S(1)}, u32[]{:S(2)}) copy-start(bf16[4,1024,192]{2,1,0:T(8,128)(2,1)S(1)} %copy.239) | copy-start | bytes 4718596
  604.5 10.8 %copy-start.14 = (bf16[9]{0:T(256)(128)(2,1)S(1)}, bf16[9]{0:T(256)(128)(2,1)}, u32[]{:S(2)}) copy-start(bf16[9]{0:T(256)(128)(2,1)} %copy-done.13) | copy-start | bytes 58
  607.2 9.2 %collective-permute-start.12 = (bf16[1,3,256,192]{2,3,1,0:T(8,128)(2,1)}, bf16[1,3,256,192]{2,3,1,0:T(8,128)(2,1)}, u32[]{:S(2)}, u32[]{:S(2)}) collective-permute-start(bf16[1,3,256,192]{2,3,1,0:T(8,128)(2,1)} %copy.240), channel_id=1, source_target_pairs={{0,16},{16,32},{32,48},{48,64},{64,80},{80,96},{96,112},{1,17},{17... | collective-permute-start | bytes 884744 | tf_op jit(solution)/shard_map/ppermute | solution.py:20
  613.4 8.2 %collective-permute-start.13 = (bf16[1,3,256,192]{2,3,1,0:T(8,128)(2,1)}, bf16[1,3,256,192]{2,3,1,0:T(8,128)(2,1)S(1)}, u32[]{:S(2)}, u32[]{:S(2)}) collective-permute-start(bf16[1,3,256,192]{2,3,1,0:T(8,128)(2,1)} %copy.242), channel_id=1, source_target_pairs={{16,0},{32,16},{48,32},{64,48},{80,64},{96,80},{112,96},{17,1},{33... | collective-permute-start | bytes 884744 | tf_op jit(solution)/shard_map/ppermute | solution.py:23
  622.7 13.3 %collective-permute-start.14 = (bf16[5,1,256,192]{2,3,1,0:T(8,128)(2,1)S(1)}, bf16[5,1,256,192]{2,3,1,0:T(8,128)(2,1)S(1)}, u32[]{:S(2)}, u32[]{:S(2)}) collective-permute-start(bf16[5,1,256,192]{2,3,1,0:T(8,128)(2,1)S(1)} %get-tuple-element.340), channel_id=1, source_target_pairs={{0,1},{1,2},{2,3},{3,4},{4,5},{5,6},{6,7},{7,8},{8,9},{9,10},{10,1... | collective-permute-start | bytes 1474568 | tf_op jit(solution)/shard_map/ppermute | solution.py:20
  624.6 13.2 %collective-permute-start.15 = (bf16[5,1,256,192]{2,3,1,0:T(8,128)(2,1)S(1)}, bf16[5,1,256,192]{2,3,1,0:T(8,128)(2,1)S(1)}, u32[]{:S(2)}, u32[]{:S(2)}) collective-permute-start(bf16[5,1,256,192]{2,3,1,0:T(8,128)(2,1)S(1)} %get-tuple-element.339), channel_id=1, source_target_pairs={{1,0},{2,1},{3,2},{4,3},{5,4},{6,5},{7,6},{8,7},{9,8},{10,9},{11,1... | collective-permute-start | bytes 1474568 | tf_op jit(solution)/shard_map/ppermute | solution.py:23
  639.1 2.4 copy-start.5
where the time goes:
time: 675 us; the launch traced here: 663 us
  local copies, waits for them, and re-layouts  346 us (51%)
  matrix products  170 us (25%)
  starting transfers between devices  55.9 us (8%)
  other arithmetic  45 us (7%)
  waiting for transfers between devices  43.2 us (6%)
    dynamic_update_slice x16, local copies, waits for them, and re-layouts, on_device(): lax.map(conv_block, (tile_taps.reshape(tile_total // tile_step, tile_step...  74.3 us
    gather x8, local copies, waits for them, and re-layouts, conv_block(): sources = group_table[block_groups]  67.5 us
    dot_general x8, matrix products, conv_block(): jnp.einsum('irtk,itkc->irtc', onehot, sources, preferred_element_type=jnp...  52.3 us
    convert_element_type x8, local copies, waits for them, and re-layouts, conv_block(): taken = jnp.einsum('irtk,itkc->irtc', onehot, sources, preferred_element_...  38.9 us
    dot_general x4, matrix products, window_block(): jnp.dot(hidden, mlp_out, preferred_element_type=jnp.float32)  37.8 us
    ppermute x8, waiting for transfers between devices, with_halo(): lax.ppermute(lax.slice_in_dim(block, block.shape[dim] - width, None, axis...  32.4 us
    ppermute x8, starting transfers between devices, with_halo(): lax.ppermute(lax.slice_in_dim(block, 0, width, axis=dim), axis, backward)  31.9 us
    dot_general x32, matrix products, one_head(): jnp.dot(weights, value_head, preferred_element_type=jnp.float32)  28 us
  transfers between devices with their start and end apart: 16, of which 9 were waited for; matrix products, arithmetic and copies ran while one was open for 5% of the time, Pallas kernels for 0%

commit v1 on v0

v1 whole, which is shorter than its diff:
```python
import functools
import math

import jax
import jax.numpy as jnp
from jax import lax
from jax.experimental import pallas as pl
from jax.experimental.pallas import tpu as pltpu
from jax.sharding import PartitionSpec as P

BF = jnp.bfloat16
F32 = jnp.float32
I32 = jnp.int32
MESH = pl.DeviceIdType.MESH

C = 192
HEADS = 8
HD = 24
HP = 32
WIN = 1024
TAPS = 27
PTS = 4096
HB = 512
CAP = PTS // 16
SLAB = CAP + CAP // 2
OFFSETS = ((-1, -1), (-1, 0), (-1, 1), (0, -1), (0, 1), (1, -1), (1, 0), (1, 1))
SEND_ORDER = (0, 7, 2, 5, 3, 4, 1, 6)
DUMP = PTS
TALL = PTS + 8
SPOT_STRIDE = 1024
SPOTS = 8 * SPOT_STRIDE
VMEM_LIMIT = 60 * 1024 * 1024
SCALE = 1.0 / math.sqrt(HD) * math.log2(math.e)
SAFE = 80.0


def params(**kw):
    return pltpu.CompilerParams(vmem_limit_bytes=VMEM_LIMIT, **kw)


VM = pl.BlockSpec(memory_space=pltpu.VMEM)
SM = pl.BlockSpec(memory_space=pltpu.SMEM)
ANY = pl.BlockSpec(memory_space=pl.ANY)


def prep_kernel(
    hp_ref, tap_ref, cw_ref, halo_ref, qkvw_ref, ow_ref, g1_ref, g2_ref, w1_ref,
    fetch_ref, sidx_ref, spot_ref, group_ref, hidx_ref, cwt_ref, qkvt_ref, owt_ref,
    g1c_ref, g2c_ref, w1t_ref, pad,
):
    ix = lax.axis_index("gx")
    iy = lax.axis_index("gy")
    ny = lax.axis_size("gy")
    hp = hp_ref[...]
    target = hp // PTS
    local = hp - target * PTS
    step_x = target // ny - ix
    step_y = target % ny - iy
    code = 3 * (step_x + 1) + (step_y + 1)
    r128 = lax.broadcasted_iota(I32, (128, 128), 0)
    c128 = lax.broadcasted_iota(I32, (128, 128), 1)
    tri = (r128 < c128).astype(F32).astype(BF)
    r32 = lax.broadcasted_iota(I32, (32, 32), 0)
    c32 = lax.broadcasted_iota(I32, (32, 32), 1)
    low = (c32 < r32).astype(F32).astype(BF)
    before = jnp.zeros((32, 128), F32)
    for c in range(9):
        if c == 4:
            continue
        m = (code == c).astype(F32)
        mb = m.astype(BF)
        within = jnp.dot(mb, tri, preferred_element_type=F32)
        above = jnp.sum(jnp.dot(low, mb, preferred_element_type=F32), 1, keepdims=True)
        before = before + m * (within + above)
    rank = before.astype(I32)
    number = code - (code > 4).astype(I32)
    own = code == 4
    fetch_ref[...] = jnp.where(own, local, PTS + number * CAP + rank)
    sidx_ref[...] = jnp.where(own, SPOTS, number * SPOT_STRIDE + rank)
    spot_ref[...] = local
    halo = halo_ref[...]
    hidx_ref[...] = jnp.where(halo < 0, DUMP, halo)

    lane = lax.broadcasted_iota(I32, (TAPS, 128), 1)
    groups = jnp.zeros((TAPS, 128), I32)
    for i in range(PTS // 128):
        top = jnp.max(tap_ref[:, i * 128 : (i + 1) * 128], 1, keepdims=True)
        groups = jnp.where(lane == i, jnp.maximum(top, 0) // 128, groups)
    group_ref[...] = groups

    for i in range(0, TAPS * C, 384):
        size = min(384, TAPS * C - i)
        cwt_ref[:, i : i + size] = cw_ref[i : i + size, :].astype(F32).T.astype(BF)

    wide = qkvw_ref[...].astype(F32).T
    pad[...] = jnp.zeros_like(pad)
    for j in range(3 * HEADS):
        pad[j * HP : j * HP + HD, :] = wide[j * HD : (j + 1) * HD, :]
    qkvt_ref[...] = pad[...].astype(BF)
    ow = ow_ref[...].astype(F32)
    for j in range(HEADS):
        pad[j * HP : j * HP + HD, :] = ow[j * HD : (j + 1) * HD, :]
    owt_ref[...] = pad[0 : HEADS * HP, :].T.astype(BF)
    g1c_ref[...] = jnp.broadcast_to(g1_ref[...], (128, C)).T
    g2c_ref[...] = jnp.broadcast_to(g2_ref[...], (128, C)).T
    w1t_ref[...] = w1_ref[...].astype(F32).T.astype(BF)


def prep(hp, tap_t, cw, halo, qkvw, ow, g1, g2, w1):
    sd = jax.ShapeDtypeStruct
    return pl.pallas_call(
        prep_kernel,
        name="prep",
        in_specs=[VM] * 9,
        out_specs=[VM] * 11,
        out_shape=[
            sd((32, 128), I32), sd((32, 128), I32), sd((32, 128), I32),
            sd((TAPS, 128), I32), sd((32, 128), I32), sd((C, TAPS * C), BF),
            sd((3 * HEADS * HP, C), BF), sd((C, HEADS * HP), BF),
            sd((C, 128), F32), sd((C, 128), F32), sd((4 * C, C), BF),
        ],
        scratch_shapes=[pltpu.VMEM((3 * HEADS * HP, C), F32)],
        compiler_params=params(),
    )(hp, tap_t, cw, halo, qkvw, ow, g1, g2, w1)


def neighbours():
    ix = lax.axis_index("gx")
    iy = lax.axis_index("gy")
    nx = lax.axis_size("gx")
    ny = lax.axis_size("gy")
    found = []
    for a, b in OFFSETS:
        x = ix + a
        y = iy + b
        inside = (x >= 0) & (x < nx) & (y >= 0) & (y < ny)
        found.append((inside, x, y))
    return found


def greet(near):
    barrier = pltpu.get_barrier_semaphore()
    for inside, x, y in near:
        @pl.when(inside)
        def _():
            pl.semaphore_signal(barrier, inc=1, device_id=(x, y), device_id_type=MESH)
    return barrier


def meet(barrier, near):
    count = sum(inside.astype(I32) for inside, _, _ in near)
    pl.semaphore_wait(barrier, count)


def push(k, near, src, dst, send_sem, recv_sem):
    _, x, y = near[k]
    return pltpu.make_async_remote_copy(
        src_ref=src, dst_ref=dst, send_sem=send_sem.at[k], recv_sem=recv_sem.at[7 - k],
        device_id=(x, y), device_id_type=MESH,
    )


def halo_kernel(idx_ref, feats_ref, out_ref, table, rows, send, zeros, send_sem, recv_sem, zero_sem):
    near = neighbours()
    barrier = greet(near)

    def turn(i, carry):
        at = pl.multiple_of(i * 128, 128)
        table[pl.ds(at, 128), :] = feats_ref[:, pl.ds(at, 128)].astype(F32).T
        return carry

    lax.fori_loop(0, PTS // 128, turn, 0)
    table[PTS:TALL, :] = jnp.zeros((TALL - PTS, C), F32)
    zeros[...] = jnp.zeros_like(zeros)
    meet(barrier, near)

    def gather(k, first, last):
        def block(b, carry):
            at = pl.multiple_of(b * 16, 16)
            got = [table[pl.ds(idx_ref[k * HB + at + u], 1), :] for u in range(16)]
            rows[pl.ds(at, 16), :] = jnp.concatenate(got, 0)
            return carry

        lax.fori_loop(first, last, block, 0)

    def start(k):
        @pl.when(near[k][0])
        def _():
            push(k, near, send.at[k], out_ref.at[7 - k], send_sem, recv_sem).start()

        @pl.when(jnp.logical_not(near[k][0]))
        def _():
            pltpu.make_async_copy(zeros, out_ref.at[k], zero_sem.at[k]).start()

    previous = None
    for k in SEND_ORDER:
        gather(k, 0, 8)
        if previous is not None:
            start(previous)
        gather(k, 8, HB // 16)
        for c in range(HB // 128):
            send[k, :, c * 128 : (c + 1) * 128] = rows[c * 128 : (c + 1) * 128, :].T.astype(BF)
        previous = k
    start(previous)

    for k in SEND_ORDER:
        @pl.when(near[k][0])
        def _():
            push(k, near, send.at[k], out_ref.at[7 - k], send_sem, recv_sem).wait_send()
            push(7 - k, near, send.at[k], out_ref.at[k], send_sem, recv_sem).wait_recv()

        @pl.when(jnp.logical_not(near[k][0]))
        def _():
            pltpu.make_async_copy(zeros, out_ref.at[k], zero_sem.at[k]).wait()


def halo_exchange(idx, feats_t):
    return pl.pallas_call(
        halo_kernel,
        name="halo_exchange",
        in_specs=[SM, VM],
        out_specs=ANY,
        out_shape=jax.ShapeDtypeStruct((8, C, HB), BF),
        scratch_shapes=[
            pltpu.VMEM((TALL, C), F32),
            pltpu.VMEM((HB, C), F32),
            pltpu.VMEM((8, C, HB), BF),
            pltpu.VMEM((C, HB), BF),
            pltpu.SemaphoreType.DMA((8,)),
            pltpu.SemaphoreType.DMA((8,)),
            pltpu.SemaphoreType.DMA((8,)),
        ],
        compiler_params=params(collective_id=0, has_side_effects=True),
    )(idx, feats_t)


STEP = 4
CONV_STEPS = PTS // (128 * STEP)


def conv_kernel(
    group_ref, fetch_ref, sidx_ref, spot_ref, tap_ref, cwt_ref, feats_ref, halo_ref,
    own_ref, slab_ref, spots_ref, lookup, gathered, table, rows, slabs, load_sem, out_sem,
):
    i = pl.program_id(0)

    @pl.when(i == 0)
    def _():
        copies = [pltpu.make_async_copy(feats_ref, lookup.at[:, 0:PTS], load_sem.at[8])]
        for k in range(8):
            at = PTS + k * HB
            copies.append(
                pltpu.make_async_copy(halo_ref.at[k], lookup.at[:, at : at + HB], load_sem.at[k])
            )
        for copy in copies:
            copy.start()

        def clear(b, carry):
            for k in range(8):
                for u in range(8):
                    spots_ref[k * SPOT_STRIDE + b * 8 + u] = DUMP
            return carry

        lax.fori_loop(0, CAP // 8, clear, 0)
        for copy in copies:
            copy.wait()

    for n in range(STEP):
        def tap(t, carry):
            start = pl.multiple_of(group_ref[t, i * STEP + n] * 128, 128)
            source = lookup[:, pl.ds(start, 128)].astype(F32)
            index = jnp.broadcast_to(tap_ref[pl.ds(t, 1), n * 128 : (n + 1) * 128], (C, 128))
            taken = jnp.take_along_axis(source, index & 127, axis=1)
            taken = jnp.where(index >= 0, taken, 0.0)
            gathered[pl.ds(pl.multiple_of(t * C, C), C), n * 128 : (n + 1) * 128] = taken.astype(BF)
            return carry

        lax.fori_loop(0, TAPS, tap, 0, unroll=True)
    conv = jnp.dot(cwt_ref[...], gathered[...], preferred_element_type=F32)
    here = lookup[:, pl.ds(pl.multiple_of(i * (128 * STEP), 128), 128 * STEP)].astype(F32)
    rows[...] = (here + conv).astype(BF).astype(F32).T

    def scatter(b, carry):
        at = b * 16
        for u in range(16):
            p = i * (128 * STEP) + at + u
            table[pl.ds(fetch_ref[p], 1), :] = rows[pl.ds(at + u, 1), :]
            spots_ref[sidx_ref[p]] = spot_ref[p]
        return carry

    lax.fori_loop(0, 8 * STEP, scatter, 0)

    @pl.when(i == CONV_STEPS - 1)
    def _():
        home = pltpu.make_async_copy(table.at[0:PTS, :], own_ref, out_sem.at[0])
        home.start()
        for k in range(8):
            at = PTS + k * CAP
            slabs[k, 0:CAP, :] = table[at : at + CAP, 0:128].astype(BF)
            half = CAP // 2
            slabs[k, CAP:SLAB, :] = jnp.concatenate(
                [table[at : at + half, 128:C], table[at + half : at + CAP, 128:C]], 1
            ).astype(BF)
        away = pltpu.make_async_copy(slabs, slab_ref, out_sem.at[1])
        away.start()
        home.wait()
        away.wait()


def conv(groups, fetch, sidx, spot, tap_t, cwt, feats_t, halo):
    sd = jax.ShapeDtypeStruct
    return pl.pallas_call(
        conv_kernel,
        name="conv",
        grid=(CONV_STEPS,),
        in_specs=[
            SM, SM, SM, SM,
            pl.BlockSpec((TAPS, 128 * STEP), lambda i: (0, i)),
            pl.BlockSpec((C, TAPS * C), lambda i: (0, 0), pipeline_mode=pl.Buffered(1)),
            ANY, ANY,
        ],
        out_specs=[ANY, ANY, SM],
        out_shape=[sd((PTS, C), F32), sd((8, SLAB, 128), BF), sd((SPOTS + 1024,), I32)],
        scratch_shapes=[
            pltpu.VMEM((C, PTS + 8 * HB), BF),
            pltpu.VMEM((TAPS * C, 128 * STEP), BF),
            pltpu.VMEM((PTS + 8 * CAP, C), F32),
            pltpu.VMEM((128 * STEP, C), F32),
            pltpu.VMEM((8, SLAB, 128), BF),
            pltpu.SemaphoreType.DMA((9,)),
            pltpu.SemaphoreType.DMA((2,)),
        ],
        compiler_params=params(dimension_semantics=("arbitrary",)),
    )(groups, fetch, sidx, spot, tap_t, cwt, feats_t, halo)


def deal_kernel(slab_ref, spots_ref, slab_out, spots_out, send_sem, recv_sem, send_spot, recv_spot):
    near = neighbours()
    barrier = greet(near)
    meet(barrier, near)

    def spot_push(k):
        src = spots_ref.at[pl.ds(k * SPOT_STRIDE, SPOT_STRIDE)]
        dst = spots_out.at[pl.ds((7 - k) * SPOT_STRIDE, SPOT_STRIDE)]
        return push(k, near, src, dst, send_spot, recv_spot)

    for k in SEND_ORDER:
        @pl.when(near[k][0])
        def _():
            push(k, near, slab_ref.at[k], slab_out.at[7 - k], send_sem, recv_sem).start()
            spot_push(k).start()

    for k in SEND_ORDER:
        @pl.when(near[k][0])
        def _():
            push(k, near, slab_ref.at[k], slab_out.at[7 - k], send_sem, recv_sem).wait_send()
            spot_push(k).wait_send()
            push(7 - k, near, slab_ref.at[k], slab_out.at[k], send_sem, recv_sem).wait_recv()
            spot_push(7 - k).wait_recv()


def deal(slabs, spots):
    sd = jax.ShapeDtypeStruct
    return pl.pallas_call(
        deal_kernel,
        name="deal",
        in_specs=[ANY, ANY],
        out_specs=[ANY, ANY],
        out_shape=[sd((8, SLAB, 128), BF), sd((SPOTS,), I32)],
        scratch_shapes=[pltpu.SemaphoreType.DMA((8,))] * 4,
        compiler_params=params(collective_id=1, has_side_effects=True),
    )(slabs, spots)


def norm_columns(values, gain):
    average = jnp.sum(values, 0, keepdims=True) * (1.0 / C)
    centred = values - average
    variance = jnp.sum(centred * centred, 0, keepdims=True) * (1.0 / C)
    return (centred * lax.rsqrt(variance + 1e-05) * gain).astype(BF)


def unpack(slab, rows, at):
    half = CAP // 2
    rows[at : at + CAP, 0:128] = slab[0:CAP, :].astype(F32)
    tail = slab[CAP:SLAB, :].astype(F32)
    rows[at : at + half, 128:C] = tail[:, 0:64]
    rows[at + half : at + CAP, 128:C] = tail[:, 64:128]


def window_kernel(
    spots_ref, own_ref, slab_ref, g1_ref, qkvt_ref, owt_ref, g2_ref, w1t_ref, w2t_ref,
    out_ref, rows, packed, attended, load_sem,
):
    home = pltpu.make_async_copy(own_ref, out_ref.at[0:PTS, :], load_sem)
    home.start()
    near = neighbours()
    for k in range(8):
        @pl.when(near[k][0])
        def _():
            unpack(slab_ref[k], rows, k * CAP)
    home.wait()
    for k in range(8):
        @pl.when(near[k][0])
        def _():
            def place(b, carry):
                at = b * 16
                for u in range(16):
                    spot = spots_ref[k * SPOT_STRIDE + at + u]
                    out_ref[pl.ds(spot, 1), :] = rows[pl.ds(k * CAP + at + u, 1), :]
                return carry

            lax.fori_loop(0, CAP // 16, place, 0)

    def window(w, carry):
        base = pl.multiple_of(w * WIN, WIN)
        x = out_ref[pl.ds(base, WIN), :].T
        normed = norm_columns(x, g1_ref[:, 0:1])
        wide = HEADS * HP
        queries = jnp.dot(qkvt_ref[0:wide, :], normed, preferred_element_type=F32) * SCALE
        packed[0:wide, :] = queries.astype(BF)
        packed[wide : 3 * wide, :] = jnp.dot(
            qkvt_ref[wide : 3 * wide, :], normed, preferred_element_type=F32
        ).astype(BF)
        largest_q = jnp.zeros((1, WIN), F32)
        largest_k = jnp.zeros((1, WIN), F32)
        for h in range(HEADS):
            q = packed[h * HP : (h + 1) * HP, :].astype(F32)
            key = packed[wide + h * HP : wide + (h + 1) * HP, :].astype(F32)
            largest_q = jnp.maximum(largest_q, jnp.sum(q * q, 0, keepdims=True))
            largest_k = jnp.maximum(largest_k, jnp.sum(key * key, 0, keepdims=True))
        safe = jnp.max(largest_q) * jnp.max(largest_k) <= SAFE * SAFE

        def heads(shifted):
            def head(h, inner):
                off = pl.multiple_of(h * HP, HP)
                q = packed[pl.ds(off, HP), :]
                key = packed[pl.ds(wide + off, HP), :]
                value = packed[pl.ds(2 * wide + off, HP), :]
                number = lax.broadcasted_iota(I32, (HP, WIN), 0)
                value = jnp.where(number == HD, jnp.ones_like(value), value)
                scores = lax.dot_general(
                    key, q, (((0,), (0,)), ((), ())), preferred_element_type=F32
                )
                if shifted:
                    scores = scores - jnp.max(scores, 0, keepdims=True)
                probs = jnp.exp2(scores).astype(BF)
                mixed = jnp.dot(value, probs, preferred_element_type=F32)
                attended[pl.ds(off, HP), :] = (mixed / mixed[HD : HD + 1, :]).astype(BF)
                return inner

            lax.fori_loop(0, HEADS, head, 0, unroll=1 if shifted else 2)

        @pl.when(safe)
        def _():
            heads(False)

        @pl.when(jnp.logical_not(safe))
        def _():
            heads(True)

        residual = x + jnp.dot(owt_ref[...], attended[...], preferred_element_type=F32)
        residual = residual.astype(BF).astype(F32)
        normed_two = norm_columns(residual, g2_ref[:, 0:1])
        hidden = jnp.dot(w1t_ref[...], normed_two, preferred_element_type=F32)
        hidden = 0.5 * hidden * (1.0 + lax.erf(hidden * (2.0**-0.5)))
        processed = residual + jnp.dot(w2t_ref[...], hidden.astype(BF), preferred_element_type=F32)
        out_ref[pl.ds(base, WIN), :] = processed.astype(BF).astype(F32).T
        return carry

    lax.fori_loop(0, PTS // WIN, window, 0)


def windows(spots, own, slabs, g1, qkvt, owt, g2, w1t, w2t):
    return pl.pallas_call(
        window_kernel,
        name="windows",
        in_specs=[SM, ANY, VM, VM, VM, VM, VM, VM, VM],
        out_specs=VM,
        out_shape=jax.ShapeDtypeStruct((TALL, C), F32),
        scratch_shapes=[
            pltpu.VMEM((8 * CAP, C), F32),
            pltpu.VMEM((3 * HEADS * HP, WIN), BF),
            pltpu.VMEM((HEADS * HP, WIN), BF),
            pltpu.SemaphoreType.DMA(()),
        ],
        compiler_params=params(),
    )(spots, own, slabs, g1, qkvt, owt, g2, w1t, w2t)


def back_kernel(spots_ref, done_ref, out_ref, rows, send, send_sem, recv_sem):
    near = neighbours()
    barrier = greet(near)
    meet(barrier, near)
    half = CAP // 2

    def gather(k, first, last):
        def block(b, carry):
            at = pl.multiple_of(b * 16, 16)
            got = [done_ref[pl.ds(spots_ref[k * SPOT_STRIDE + at + u], 1), :] for u in range(16)]
            rows[pl.ds(at, 16), :] = jnp.concatenate(got, 0)
            return carry

        lax.fori_loop(first, last, block, 0)

    def start(k):
        @pl.when(near[k][0])
        def _():
            push(k, near, send.at[k], out_ref.at[7 - k], send_sem, recv_sem).start()

    previous = None
    for k in SEND_ORDER:
        @pl.when(near[k][0])
        def _():
            gather(k, 0, 4)

        if previous is not None:
            start(previous)

        @pl.when(near[k][0])
        def _():
            gather(k, 4, CAP // 16)
            send[k, 0:CAP, :] = rows[:, 0:128].astype(BF)
            send[k, CAP:SLAB, :] = jnp.concatenate(
                [rows[0:half, 128:C], rows[half:CAP, 128:C]], 1
            ).astype(BF)

        previous = k
    start(previous)

    for k in SEND_ORDER:
        @pl.when(near[k][0])
        def _():
            push(k, near, send.at[k], out_ref.at[7 - k], send_sem, recv_sem).wait_send()
            push(7 - k, near, send.at[k], out_ref.at[k], send_sem, recv_sem).wait_recv()


def back(spots, done):
    return pl.pallas_call(
        back_kernel,
        name="back",
        in_specs=[SM, VM],
        out_specs=ANY,
        out_shape=jax.ShapeDtypeStruct((8, SLAB, 128), BF),
        scratch_shapes=[
            pltpu.VMEM((CAP, C), F32),
            pltpu.VMEM((8, SLAB, 128), BF),
            pltpu.SemaphoreType.DMA((8,)),
            pltpu.SemaphoreType.DMA((8,)),
        ],
        compiler_params=params(collective_id=2, has_side_effects=True),
    )(spots, done)


def collect_kernel(fetch_ref, done_ref, slab_ref, out_ref, table, rows, load_sem):
    home = pltpu.make_async_copy(done_ref.at[0:PTS, :], table.at[0:PTS, :], load_sem)
    home.start()
    near = neighbours()
    for k in range(8):
        @pl.when(near[k][0])
        def _():
            unpack(slab_ref[k], table, PTS + k * CAP)
    home.wait()

    def tile(i, carry):
        def block(b, inner):
            at = pl.multiple_of(b * 16, 16)
            got = [table[pl.ds(fetch_ref[i * 128 + at + u], 1), :] for u in range(16)]
            rows[pl.ds(at, 16), :] = jnp.concatenate(got, 0)
            return inner

        lax.fori_loop(0, 8, block, 0)
        out_ref[:, pl.ds(pl.multiple_of(i * 128, 128), 128)] = rows[...].T.astype(BF)
        return carry

    lax.fori_loop(0, PTS // 128, tile, 0)


def collect(fetch, done, slabs):
    return pl.pallas_call(
        collect_kernel,
        name="collect",
        in_specs=[SM, ANY, VM],
        out_specs=VM,
        out_shape=jax.ShapeDtypeStruct((C, PTS), BF),
        scratch_shapes=[
            pltpu.VMEM((PTS + 8 * CAP, C), F32),
            pltpu.VMEM((128, C), F32),
            pltpu.SemaphoreType.DMA(()),
        ],
        compiler_params=params(),
    )(fetch, done, slabs)


def on_device(
    feats, conv_weight, tap_index, halo_rows, hilbert_pos,
    ln1_gain, qkv_weight, out_weight, ln2_gain, mlp_in, mlp_out,
):
    feats_t = feats.T
    tap_t = tap_index.T
    fetch, sidx, spot, groups, hidx, cwt, qkvt, owt, g1, g2, w1t = prep(
        hilbert_pos.reshape(32, 128), tap_t, conv_weight.reshape(TAPS * C, C),
        halo_rows.reshape(32, 128), qkv_weight, out_weight,
        ln1_gain.reshape(1, C), ln2_gain.reshape(1, C), mlp_in,
    )
    fetch, sidx, spot, hidx = (a.reshape(PTS) for a in (fetch, sidx, spot, hidx))
    halo = halo_exchange(hidx, feats_t)
    own, slabs, spots = conv(groups, fetch, sidx, spot, tap_t, cwt, feats_t, halo)
    slabs, spots = deal(slabs, spots)
    done = windows(spots, own, slabs, g1, qkvt, owt, g2, w1t, mlp_out.T)
    arrived = back(spots, done)
    return collect(fetch, done, arrived).T


def solution(mesh):
    rows = P(("gx", "gy"), None)
    placed = (rows, P(), rows, P(("gx", "gy"), None, None), P(("gx", "gy"))) + (P(),) * 6
    return jax.shard_map(
        on_device, mesh=mesh, in_specs=placed, out_specs=rows, check_vma=False
    )
```

time: 675 us -> 201 us (0.30); the launches traced: 663 us -> 198 us
  local copies, waits for them, and re-layouts: 346 us -> 1.32 us
  Pallas kernels: 0 us -> 197 us
  matrix products: 170 us -> 0 us
  starting transfers between devices: 55.9 us -> 0 us
  other arithmetic: 45 us -> 0 us
  waiting for transfers between devices: 43.2 us -> 0 us
    pallas_call x0 -> x7, Pallas kernels: none -> 197 us  [the longest x1 72.3 us: windows(): pl.pallas_call(window_kernel, name='windows', in_specs=[SM, ANY, VM, VM,...]
    dot_general x92 -> x0, matrix products: 170 us -> none  [the longest x8 52.3 us: conv_block(): jnp.einsum('irtk,itkc->irtc', onehot, sources, preferred_element_type=jnp...]
    gather x13 -> x0, local copies, waits for them, and re-layouts: 116 us -> none  [the longest x8 67.5 us: conv_block(): sources = group_table[block_groups]]
    dynamic_update_slice x16 -> x0, local copies, waits for them, and re-layouts: 74.3 us -> none  [on_device(): lax.map(conv_block, (tile_taps.reshape(tile_total // tile_step, tile_step...]
    scatter x3 -> x0, local copies, waits for them, and re-layouts: 61.3 us -> none  [the longest x1 27.3 us: on_device(): ordered = jnp.zeros((points + 1, channels), jnp.bfloat16).at[jnp.concaten...]
    ppermute x16 -> x0, starting transfers between devices: 55.9 us -> none  [the longest x8 31.9 us: with_halo(): lax.ppermute(lax.slice_in_dim(block, 0, width, axis=dim), axis, backward)]
    ppermute x16 -> x0, waiting for transfers between devices: 43.2 us -> none  [the longest x8 32.4 us: with_halo(): lax.ppermute(lax.slice_in_dim(block, block.shape[dim] - width, None, axis...]
    convert_element_type x9 -> x0, local copies, waits for them, and re-layouts: 41.4 us -> none  [the longest x8 38.9 us: conv_block(): taken = jnp.einsum('irtk,itkc->irtc', onehot, sources, preferred_element_...]
  transfers between devices with their start and end apart: 16 -> 0, of which waited for: 9 -> 0; matrix products, arithmetic and copies ran while one was open for 5% -> 0% of each run, Pallas kernels for 0% -> 0%
where the time goes in v1:
time: 201 us; the launch traced here: 198 us
  Pallas kernels  197 us (98%)
    pallas_call x1, Pallas kernels, windows(): pl.pallas_call(window_kernel, name='windows', in_specs=[SM, ANY, VM, VM,...  72.3 us
    pallas_call x1, Pallas kernels, conv(): pl.pallas_call(conv_kernel, name='conv', grid=(CONV_STEPS,), in_specs=[SM...  50.5 us
    pallas_call x1, Pallas kernels, halo_exchange(): pl.pallas_call(halo_kernel, name='halo_exchange', in_specs=[SM, VM], out_...  24.2 us
    pallas_call x1, Pallas kernels, collect(): pl.pallas_call(collect_kernel, name='collect', in_specs=[SM, ANY, VM], ou...  16.8 us
    pallas_call x1, Pallas kernels, back(): pl.pallas_call(back_kernel, name='back', in_specs=[SM, VM], out_specs=ANY...  16.4 us
    pallas_call x1, Pallas kernels, deal(): pl.pallas_call(deal_kernel, name='deal', in_specs=[ANY, ANY], out_specs=[...  11.4 us
    pallas_call x1, Pallas kernels, prep(): pl.pallas_call(prep_kernel, name='prep', in_specs=[VM] * 9, out_specs=[VM...  5.21 us

profile of v1, /device:TPU:25, one launch (start us, length us, event | category | flops | bytes accessed | tf_op | source)
XLA Modules:
  0.0 198.3 jit_solution(2576386282411396983)
XLA Ops:
  0.0 1.3 reshape.29.halo_ref
  1.3 5.2 %prep.1 = (s32[32,128]{1,0:T(8,128)}, s32[32,128]{1,0:T(8,128)}, s32[32,128]{1,0:T(8,128)}, s32[27,128]{1,0:T(8,128)}, s32[32,128]{1,0:T(8,128)}, /*index=5*/bf1...) custom-call(s32[32,128]{1,0:T(8,128)} %bitcast.20, ...), custom_call_target="tpu_custom_call" | custom-call | tf_op jit(solution)/shard_map/prep/pallas_call | solution.py:111
  6.5 24.2 %halo_exchange.1.halo_ref = bf16[8,192,512]{2,1,0:T(8,128)(2,1)} custom-call(s32[4096]{0:T(1024)} %bitcast.23, bf16[192,4096]{1,0:T(8,128)(2,1)} %bitcast.12), custom_call_target="tpu_custom_call" | custom-call | tf_op jit(solution)/shard_map/halo_exchange/pallas_call | solution.py:218
  30.7 50.5 %conv.1 = (f32[4096,192]{1,0:T(8,128)}, bf16[8,384,128]{2,1,0:T(8,128)(2,1)}, s32[9216]{0:T(1024)}) custom-call(s32[27,128]{1,0:T(8,128)} %get-tuple-element.22.group_ref, s32[4096]{0:T(1024)} %bitcast.18, s32[4096]{0:T(1024)} %bitcast.21, s32[4096]{0:T(1024)} %bitcast.22, s32[27,4096]{1,0:T(8,128)} %bitcast.16, ...), custom_call_target="tpu_custom_call" | custom-call | tf_op jit(solution)/shard_map/conv/pallas_call | solution.py:312
  81.3 11.4 %deal.1 = (bf16[8,384,128]{2,1,0:T(8,128)(2,1)}, s32[8192]{0:T(1024)}) custom-call(bf16[8,384,128]{2,1,0:T(8,128)(2,1)} %get-tuple-element.27.slab_ref, s32[9216]{0:T(1024)} %get-tuple-element.28.spots_ref), custom_call_target="tpu_custom_call" | custom-call | tf_op jit(solution)/shard_map/deal/pallas_call | solution.py:364
  92.6 72.3 %windows.1.done_ref = f32[4104,192]{1,0:T(8,128)} custom-call(s32[8192]{0:T(1024)} %get-tuple-element.29.spots_ref, f32[4096,192]{1,0:T(8,128)} %get-tuple-element.30.own_ref, bf16[8,384,128]{2,1,0:T(8,128)(2,1)} %get-tuple-element.31.slab_ref, f32[192,128]{1,0:T(8,128)} %get-tuple-element.32.g1_ref, bf16[768,192]{1,0:T(8,128)(2,1)} %get-tuple-element.33.qkvt_ref, ...), custom_call_target="tpu_custom_call" | custom-call | tf_op jit(solution)/shard_map/windows/pallas_call | solution.py:474
  164.9 16.4 %back.1.slab_ref = bf16[8,384,128]{2,1,0:T(8,128)(2,1)} custom-call(s32[8192]{0:T(1024)} %get-tuple-element.29.spots_ref, f32[4104,192]{1,0:T(8,128)} %windows.1.done_ref), custom_call_target="tpu_custom_call" | custom-call | tf_op jit(solution)/shard_map/back/pallas_call | solution.py:538
  181.3 16.8 %collect.1 = bf16[192,4096]{1,0:T(8,128)(2,1)} custom-call(s32[4096]{0:T(1024)} %bitcast.19, f32[4104,192]{1,0:T(8,128)} %windows.1.done_ref, bf16[8,384,128]{2,1,0:T(8,128)(2,1)} %back.1.slab_ref), custom_call_target="tpu_custom_call" | custom-call | tf_op jit(solution)/shard_map/collect/pallas_call | solution.py:579

commit v2 on v1

v2 whole, which is shorter than its diff:
```python
import functools
import math

import jax
import jax.numpy as jnp
from jax import lax
from jax.experimental import pallas as pl
from jax.experimental.pallas import tpu as pltpu
from jax.sharding import PartitionSpec as P

BF = jnp.bfloat16
F32 = jnp.float32
I32 = jnp.int32
MESH = pl.DeviceIdType.MESH

C = 192
HEADS = 8
HD = 24
HP = 32
WIN = 1024
TAPS = 27
PTS = 4096
HB = 512
CAP = PTS // 16
GROUP = 128
SLOTS = PTS + 8 * CAP
ROWS = C + 16
VMEM_LIMIT = 60 * 1024 * 1024
SCALE = 1.0 / math.sqrt(HD) * math.log2(math.e)
SAFE = 80.0


def params(**kw):
    return pltpu.CompilerParams(vmem_limit_bytes=VMEM_LIMIT, **kw)


VM = pl.BlockSpec(memory_space=pltpu.VMEM)
SM = pl.BlockSpec(memory_space=pltpu.SMEM)
ANY = pl.BlockSpec(memory_space=pl.ANY)


def neighbour(k):
    j = k + k // 4
    x = lax.axis_index("gx") + j // 3 - 1
    y = lax.axis_index("gy") + j % 3 - 1
    inside = (x >= 0) & (x < lax.axis_size("gx")) & (y >= 0) & (y < lax.axis_size("gy"))
    return inside, x, y


def in_turn(i):
    return i + jnp.minimum(i, 1) - 3 * (i // 3)


def greet():
    barrier = pltpu.get_barrier_semaphore()
    count = jnp.int32(0)
    for k in range(8):
        inside, x, y = neighbour(k)
        count = count + inside.astype(I32)

        @pl.when(inside)
        def _():
            pl.semaphore_signal(barrier, inc=1, device_id=(x, y), device_id_type=MESH)

    return barrier, count


def push(k, src, dst, send_sem, recv_sem):
    _, x, y = neighbour(k)
    return pltpu.make_async_remote_copy(
        src_ref=src, dst_ref=dst, send_sem=send_sem.at[k], recv_sem=recv_sem.at[7 - k],
        device_id=(x, y), device_id_type=MESH,
    )


def each(body):
    def step(k, carry):
        body(k)
        return carry

    lax.fori_loop(0, 8, step, 0)


def index_row(ref, first, count):
    return jnp.concatenate([ref[pl.ds(first + u, 1), :] for u in range(count)], 1)


def select_columns(index, onehot):
    depth, width = onehot.shape
    for s in range(0, depth, 256):
        place = lax.broadcasted_iota(I32, (256, width), 0) + s
        onehot[s : s + 256, :] = jnp.where(place == index, 1.0, 0.0).astype(BF)


def prepare_indices(hp_ref, tap_ref, fetch_ref, own_ref, away_ref, spot_ref, group_ref, blank_ref):
    ix = lax.axis_index("gx")
    iy = lax.axis_index("gy")
    ny = lax.axis_size("gy")
    hp = hp_ref[...]
    target = hp // PTS
    local = hp - target * PTS
    step_x = target // ny - ix
    step_y = target % ny - iy
    code = 3 * (step_x + 1) + (step_y + 1)
    r128 = lax.broadcasted_iota(I32, (128, 128), 0)
    c128 = lax.broadcasted_iota(I32, (128, 128), 1)
    tri = (r128 < c128).astype(F32).astype(BF)
    r32 = lax.broadcasted_iota(I32, (32, 32), 0)
    c32 = lax.broadcasted_iota(I32, (32, 32), 1)
    low = (c32 < r32).astype(F32).astype(BF)
    before = jnp.zeros((32, 128), F32)
    for c in range(9):
        if c == 4:
            continue
        m = (code == c).astype(F32)
        mb = m.astype(BF)
        within = jnp.dot(mb, tri, preferred_element_type=F32)
        above = jnp.sum(jnp.dot(low, mb, preferred_element_type=F32), 1, keepdims=True)
        before = before + m * (within + above)
    away = (code - (code > 4).astype(I32)) * CAP + before.astype(I32)
    own = code == 4
    fetch_ref[...] = jnp.where(own, local, PTS + away)
    own_ref[...] = jnp.where(own, local, -1)
    away_ref[...] = jnp.where(own, -1, away)
    spot_ref[...] = local
    blank_ref[...] = jnp.full_like(blank_ref, -1)
    lane = lax.broadcasted_iota(I32, (TAPS, 128), 1)
    groups = jnp.zeros((TAPS, 128), I32)
    for i in range(PTS // 128):
        top = jnp.max(tap_ref[:, i * 128 : (i + 1) * 128], 1, keepdims=True)
        groups = jnp.where(lane == i, jnp.maximum(top, 0) // 128, groups)
    group_ref[...] = groups


def prepare_weights(
    cw_ref, qkvw_ref, ow_ref, g1_ref, g2_ref, w1_ref, cwt_ref, qkvt_ref, owt_ref, g1c_ref, g2c_ref, w1t_ref, pad
):
    for i in range(0, TAPS * C, 384):
        size = min(384, TAPS * C - i)
        cwt_ref[:, i : i + size] = cw_ref[i : i + size, :].astype(F32).T.astype(BF)
    wide = qkvw_ref[...].astype(F32).T
    pad[...] = jnp.zeros_like(pad)
    for j in range(3 * HEADS):
        pad[j * HP : j * HP + HD, :] = wide[j * HD : (j + 1) * HD, :]
    qkvt_ref[...] = pad[...].astype(BF)
    ow = ow_ref[...].astype(F32)
    for j in range(HEADS):
        pad[j * HP : j * HP + HD, :] = ow[j * HD : (j + 1) * HD, :]
    owt_ref[...] = pad[0 : HEADS * HP, :].T.astype(BF)
    g1c_ref[...] = jnp.broadcast_to(g1_ref[...], (128, C)).T
    g2c_ref[...] = jnp.broadcast_to(g2_ref[...], (128, C)).T
    w1t_ref[...] = w1_ref[...].astype(F32).T.astype(BF)


def halo_kernel(
    halo_ref, feats_ref, hp_ref, tap_ref, cw_ref, qkvw_ref, ow_ref, g1_ref, g2_ref, w1_ref,
    out_ref, fetch_ref, own_ref, away_ref, spot_ref, group_ref, blank_ref,
    cwt_ref, qkvt_ref, owt_ref, g1c_ref, g2c_ref, w1t_ref,
    onehot_a, onehot_b, send, zeros, pad, send_sem, recv_sem, zero_sem,
):
    barrier, count = greet()
    zeros[...] = jnp.zeros_like(zeros)

    def start(k):
        inside = neighbour(k)[0]

        @pl.when(inside)
        def _():
            push(k, send.at[k], out_ref.at[7 - k], send_sem, recv_sem).start()

        @pl.when(jnp.logical_not(inside))
        def _():
            pltpu.make_async_copy(zeros, out_ref.at[k], zero_sem.at[k]).start()

    pl.semaphore_wait(barrier, count)

    def pair(i, carry):
        k = in_turn(i)
        select_columns(halo_ref[pl.ds(k, 1), :], onehot_a)
        select_columns(halo_ref[pl.ds(7 - k, 1), :], onehot_b)

        @pl.when(i > 0)
        def _():
            start(7 - in_turn(i - 1))

        send[k] = jnp.dot(feats_ref[...], onehot_a[...], preferred_element_type=F32).astype(BF)
        send[7 - k] = jnp.dot(feats_ref[...], onehot_b[...], preferred_element_type=F32).astype(BF)
        start(k)
        return carry

    lax.fori_loop(0, 4, pair, 0)
    prepare_indices(hp_ref, tap_ref, fetch_ref, own_ref, away_ref, spot_ref, group_ref, blank_ref)
    start(7 - in_turn(3))
    prepare_weights(
        cw_ref, qkvw_ref, ow_ref, g1_ref, g2_ref, w1_ref,
        cwt_ref, qkvt_ref, owt_ref, g1c_ref, g2c_ref, w1t_ref, pad,
    )

    def finish(k):
        inside = neighbour(k)[0]

        @pl.when(inside)
        def _():
            push(k, send.at[k], out_ref.at[7 - k], send_sem, recv_sem).wait_send()
            push(7 - k, send.at[k], out_ref.at[k], send_sem, recv_sem).wait_recv()

        @pl.when(jnp.logical_not(inside))
        def _():
            pltpu.make_async_copy(zeros, out_ref.at[k], zero_sem.at[k]).wait()

    each(finish)


def halo_exchange(halo, feats_t, hp, tap_t, cw, qkvw, ow, g1, g2, w1):
    sd = jax.ShapeDtypeStruct
    return pl.pallas_call(
        halo_kernel,
        name="halo_exchange",
        in_specs=[VM] * 10,
        out_specs=[ANY] + [VM] * 12,
        out_shape=[
            sd((8, C, HB), BF),
            sd((32, 128), I32), sd((32, 128), I32), sd((32, 128), I32), sd((32, 128), I32),
            sd((TAPS, 128), I32), sd((SLOTS // 128, 128), I32),
            sd((C, TAPS * C), BF), sd((3 * HEADS * HP, C), BF), sd((C, HEADS * HP), BF),
            sd((C, 128), F32), sd((C, 128), F32), sd((4 * C, C), BF),
        ],
        scratch_shapes=[
            pltpu.VMEM((PTS, HB), BF),
            pltpu.VMEM((PTS, HB), BF),
            pltpu.VMEM((8, C, HB), BF),
            pltpu.VMEM((C, HB), BF),
            pltpu.VMEM((3 * HEADS * HP, C), F32),
            pltpu.SemaphoreType.DMA((8,)),
            pltpu.SemaphoreType.DMA((8,)),
            pltpu.SemaphoreType.DMA((8,)),
        ],
        compiler_params=params(collective_id=0, has_side_effects=True),
    )(halo, feats_t, hp, tap_t, cw, qkvw, ow, g1, g2, w1)


STEP = 4
CONV_STEPS = PTS // (128 * STEP)


def conv_kernel(
    group_ref, fetch_ref, spot_ref, tap_ref, cwt_ref, feats_ref, halo_ref, blank_ref,
    out_ref, source_ref, lookup, gathered, load_sem,
):
    i = pl.program_id(0)

    @pl.when(i == 0)
    def _():
        copies = [
            pltpu.make_async_copy(blank_ref, source_ref, load_sem.at[9]),
            pltpu.make_async_copy(feats_ref, lookup.at[:, 0:PTS], load_sem.at[8]),
        ]
        for k in range(8):
            at = PTS + k * HB
            copies.append(
                pltpu.make_async_copy(halo_ref.at[k], lookup.at[:, at : at + HB], load_sem.at[k])
            )
        for copy in copies:
            copy.start()
        for copy in copies:
            copy.wait()

    for n in range(STEP):
        def tap(t, carry):
            start = pl.multiple_of(group_ref[t, i * STEP + n] * 128, 128)
            source = lookup[:, pl.ds(start, 128)].astype(F32)
            index = jnp.broadcast_to(tap_ref[pl.ds(t, 1), n * 128 : (n + 1) * 128], (C, 128))
            taken = jnp.take_along_axis(source, index & 127, axis=1)
            taken = jnp.where(index >= 0, taken, 0.0)
            gathered[pl.ds(pl.multiple_of(t * C, C), C), n * 128 : (n + 1) * 128] = taken.astype(BF)
            return carry

        lax.fori_loop(0, TAPS, tap, 0, unroll=True)

    def note(b, carry):
        for u in range(32):
            p = i * (128 * STEP) + b * 32 + u
            source_ref[fetch_ref[p]] = p
        return carry

    lax.fori_loop(0, 4 * STEP, note, 0)
    conv = jnp.dot(cwt_ref[...], gathered[...], preferred_element_type=F32)
    here = lookup[:, pl.ds(pl.multiple_of(i * (128 * STEP), 128), 128 * STEP)].astype(F32)
    out_ref[0:C, :] = (here + conv).astype(BF)
    spot = index_row(spot_ref, 0, STEP) + 1
    number = lax.broadcasted_iota(I32, (ROWS - C, 128 * STEP), 0)
    digits = jnp.where(number == 0, spot // 64, jnp.where(number == 1, spot % 64, 0))
    out_ref[C:ROWS, :] = digits.astype(F32).astype(BF)


def conv(groups, fetch, spot, tap_t, cwt, feats_t, halo, blank):
    sd = jax.ShapeDtypeStruct
    return pl.pallas_call(
        conv_kernel,
        name="conv",
        grid=(CONV_STEPS,),
        in_specs=[
            SM, SM,
            pl.BlockSpec((None, STEP, 128), lambda i: (i, 0, 0)),
            pl.BlockSpec((TAPS, 128 * STEP), lambda i: (0, i)),
            pl.BlockSpec((C, TAPS * C), lambda i: (0, 0), pipeline_mode=pl.Buffered(1)),
            ANY, ANY, ANY,
        ],
        out_specs=[pl.BlockSpec((ROWS, 128 * STEP), lambda i: (0, i)), SM],
        out_shape=[sd((ROWS, PTS), BF), sd((SLOTS,), I32)],
        scratch_shapes=[
            pltpu.VMEM((C, PTS + 8 * HB), BF),
            pltpu.VMEM((TAPS * C, 128 * STEP), BF),
            pltpu.SemaphoreType.DMA((10,)),
        ],
        compiler_params=params(dimension_semantics=("arbitrary",)),
    )(groups, fetch, spot, tap_t, cwt, feats_t, halo, blank)


BLOCK = 512


def deal_kernel(updated_ref, source_ref, out_ref, spots_ref, onehot_a, onehot_b, send, recv, send_sem, recv_sem):
    barrier, count = greet()

    def blank(k):
        @pl.when(jnp.logical_not(neighbour(k)[0]))
        def _():
            recv[k] = jnp.zeros((ROWS, CAP), BF)

    each(blank)

    def start(k):
        @pl.when(neighbour(k)[0])
        def _():
            push(k, send.at[k], recv.at[7 - k], send_sem, recv_sem).start()

    pl.semaphore_wait(barrier, count)
    first = onehot_a.at[:, 0:CAP]
    second = onehot_b.at[:, 0:CAP]

    def pair(i, carry):
        k = in_turn(i)
        base = PTS // 128
        select_columns(index_row(source_ref, base + k * (CAP // 128), CAP // 128), first)
        select_columns(index_row(source_ref, base + (7 - k) * (CAP // 128), CAP // 128), second)

        @pl.when(i > 0)
        def _():
            start(7 - in_turn(i - 1))

        send[k] = jnp.dot(updated_ref[...], first[...], preferred_element_type=F32).astype(BF)
        send[7 - k] = jnp.dot(updated_ref[...], second[...], preferred_element_type=F32).astype(BF)
        start(k)
        return carry

    lax.fori_loop(0, 4, pair, 0)

    def stay(n, carry):
        select_columns(index_row(source_ref, n * (BLOCK // 128), BLOCK // 128), onehot_a)

        @pl.when(n == 0)
        def _():
            start(7 - in_turn(3))

        taken = jnp.dot(updated_ref[0:C, :], onehot_a[...], preferred_element_type=F32)
        out_ref[:, pl.ds(pl.multiple_of(n * BLOCK, BLOCK), BLOCK)] = taken.astype(BF)
        return carry

    lax.fori_loop(0, PTS // BLOCK, stay, 0)

    def finish(k):
        @pl.when(neighbour(k)[0])
        def _():
            push(k, send.at[k], recv.at[7 - k], send_sem, recv_sem).wait_send()
            push(7 - k, send.at[k], recv.at[k], send_sem, recv_sem).wait_recv()

    each(finish)

    for k in range(8):
        digits = recv[k, C:ROWS, :].astype(F32)
        spots_ref[k : k + 1, :] = (digits[0:1, :] * 64.0 + digits[1:2, :] - 1.0).astype(I32)

    def arrive(n, carry):
        total = jnp.zeros((C, BLOCK), F32)
        at = pl.multiple_of(n * BLOCK, BLOCK)
        place = lax.broadcasted_iota(I32, (BLOCK, CAP), 0) + at
        for k in range(8):
            chosen = jnp.where(place == spots_ref[k : k + 1, :], 1.0, 0.0).astype(BF)
            total = total + lax.dot_general(
                recv[k, 0:C, :], chosen, (((1,), (1,)), ((), ())), preferred_element_type=F32
            )
        here = out_ref[:, pl.ds(at, BLOCK)].astype(F32) + total
        out_ref[:, pl.ds(at, BLOCK)] = here.astype(BF)
        return carry

    lax.fori_loop(0, PTS // BLOCK, arrive, 0)


def deal(updated, source):
    sd = jax.ShapeDtypeStruct
    return pl.pallas_call(
        deal_kernel,
        name="deal",
        in_specs=[VM, VM],
        out_specs=[VM, VM],
        out_shape=[sd((C, PTS), BF), sd((8, CAP), I32)],
        scratch_shapes=[
            pltpu.VMEM((PTS, BLOCK), BF),
            pltpu.VMEM((PTS, BLOCK), BF),
            pltpu.VMEM((8, ROWS, CAP), BF),
            pltpu.VMEM((8, ROWS, CAP), BF),
            pltpu.SemaphoreType.DMA((8,)),
            pltpu.SemaphoreType.DMA((8,)),
        ],
        compiler_params=params(collective_id=1, has_side_effects=True),
    )(updated, source)


def norm_columns(values, gain):
    average = jnp.sum(values, 0, keepdims=True) * (1.0 / C)
    centred = values - average
    variance = jnp.sum(centred * centred, 0, keepdims=True) * (1.0 / C)
    return (centred * lax.rsqrt(variance + 1e-05) * gain).astype(BF)


def window_kernel(
    in_ref, g1_ref, qkvt_ref, owt_ref, g2_ref, w1t_ref, w2t_ref, out_ref, packed, attended
):
    def window(w, carry):
        base = pl.multiple_of(w * WIN, WIN)
        x = in_ref[:, pl.ds(base, WIN)].astype(F32)
        normed = norm_columns(x, g1_ref[:, 0:1])
        wide = HEADS * HP
        queries = jnp.dot(qkvt_ref[0:wide, :], normed, preferred_element_type=F32) * SCALE
        packed[0:wide, :] = queries.astype(BF)
        packed[wide : 3 * wide, :] = jnp.dot(
            qkvt_ref[wide : 3 * wide, :], normed, preferred_element_type=F32
        ).astype(BF)
        largest_q = jnp.zeros((1, WIN), F32)
        largest_k = jnp.zeros((1, WIN), F32)
        for h in range(HEADS):
            q = packed[h * HP : (h + 1) * HP, :].astype(F32)
            key = packed[wide + h * HP : wide + (h + 1) * HP, :].astype(F32)
            largest_q = jnp.maximum(largest_q, jnp.sum(q * q, 0, keepdims=True))
            largest_k = jnp.maximum(largest_k, jnp.sum(key * key, 0, keepdims=True))
        safe = jnp.max(largest_q) * jnp.max(largest_k) <= SAFE * SAFE

        def heads(shifted):
            def head(h, inner):
                off = pl.multiple_of(h * HP, HP)
                q = packed[pl.ds(off, HP), :]
                key = packed[pl.ds(wide + off, HP), :]
                value = packed[pl.ds(2 * wide + off, HP), :]
                number = lax.broadcasted_iota(I32, (HP, WIN), 0)
                value = jnp.where(number == HD, jnp.ones_like(value), value)
                scores = lax.dot_general(
                    key, q, (((0,), (0,)), ((), ())), preferred_element_type=F32
                )
                if shifted:
                    scores = scores - jnp.max(scores, 0, keepdims=True)
                probs = jnp.exp2(scores).astype(BF)
                mixed = jnp.dot(value, probs, preferred_element_type=F32)
                attended[pl.ds(off, HP), :] = (mixed / mixed[HD : HD + 1, :]).astype(BF)
                return inner

            lax.fori_loop(0, HEADS, head, 0, unroll=1 if shifted else 2)

        @pl.when(safe)
        def _():
            heads(False)

        @pl.when(jnp.logical_not(safe))
        def _():
            heads(True)

        residual = x + jnp.dot(owt_ref[...], attended[...], preferred_element_type=F32)
        residual = residual.astype(BF).astype(F32)
        normed_two = norm_columns(residual, g2_ref[:, 0:1])
        hidden = jnp.dot(w1t_ref[...], normed_two, preferred_element_type=F32)
        hidden = 0.5 * hidden * (1.0 + lax.erf(hidden * (2.0**-0.5)))
        processed = residual + jnp.dot(w2t_ref[...], hidden.astype(BF), preferred_element_type=F32)
        out_ref[:, pl.ds(base, WIN)] = processed.astype(BF)
        return carry

    lax.fori_loop(0, PTS // WIN, window, 0)


def windows(ordered, g1, qkvt, owt, g2, w1t, w2t):
    return pl.pallas_call(
        window_kernel,
        name="windows",
        in_specs=[VM] * 7,
        out_specs=VM,
        out_shape=jax.ShapeDtypeStruct((C, PTS), BF),
        scratch_shapes=[
            pltpu.VMEM((3 * HEADS * HP, WIN), BF),
            pltpu.VMEM((HEADS * HP, WIN), BF),
        ],
        compiler_params=params(),
    )(ordered, g1, qkvt, owt, g2, w1t, w2t)


def back_kernel(done_ref, spots_ref, own_ref, away_ref, out_ref, onehot_a, onehot_b, send, recv, send_sem, recv_sem):
    barrier, count = greet()

    def landing(k):
        return recv.at[:, pl.ds(pl.multiple_of(k * CAP, CAP), CAP)]

    def blank(k):
        @pl.when(jnp.logical_not(neighbour(k)[0]))
        def _():
            recv[:, pl.ds(pl.multiple_of(k * CAP, CAP), CAP)] = jnp.zeros((C, CAP), BF)

    each(blank)

    def start(k):
        @pl.when(neighbour(k)[0])
        def _():
            push(k, send.at[k], landing(7 - k), send_sem, recv_sem).start()

    pl.semaphore_wait(barrier, count)
    first = onehot_a.at[:, 0:CAP]
    second = onehot_b.at[:, 0:CAP]

    def pair(i, carry):
        k = in_turn(i)
        select_columns(spots_ref[pl.ds(k, 1), :], first)
        select_columns(spots_ref[pl.ds(7 - k, 1), :], second)

        @pl.when(i > 0)
        def _():
            start(7 - in_turn(i - 1))

        send[k] = jnp.dot(done_ref[...], first[...], preferred_element_type=F32).astype(BF)
        send[7 - k] = jnp.dot(done_ref[...], second[...], preferred_element_type=F32).astype(BF)
        start(k)
        return carry

    lax.fori_loop(0, 4, pair, 0)

    def stay(n, carry):
        select_columns(index_row(own_ref, n * (BLOCK // 128), BLOCK // 128), onehot_a)

        @pl.when(n == 0)
        def _():
            start(7 - in_turn(3))

        taken = jnp.dot(done_ref[...], onehot_a[...], preferred_element_type=F32)
        out_ref[:, pl.ds(pl.multiple_of(n * BLOCK, BLOCK), BLOCK)] = taken.astype(BF)
        return carry

    lax.fori_loop(0, PTS // BLOCK, stay, 0)

    def finish(k):
        @pl.when(neighbour(k)[0])
        def _():
            push(k, send.at[k], landing(7 - k), send_sem, recv_sem).wait_send()
            push(7 - k, send.at[k], landing(k), send_sem, recv_sem).wait_recv()

    each(finish)
    depth = 8 * CAP

    def returned(n, onehot):
        select_columns(index_row(away_ref, n * (BLOCK // 128), BLOCK // 128), onehot.at[0:depth, :])

    def add(n, onehot):
        taken = jnp.dot(recv[...], onehot[0:depth, :], preferred_element_type=F32)
        at = pl.multiple_of(n * BLOCK, BLOCK)
        here = out_ref[:, pl.ds(at, BLOCK)].astype(F32) + taken
        out_ref[:, pl.ds(at, BLOCK)] = here.astype(BF)

    def last(m, carry):
        returned(2 * m, onehot_a)
        returned(2 * m + 1, onehot_b)
        add(2 * m, onehot_a)
        add(2 * m + 1, onehot_b)
        return carry

    lax.fori_loop(0, PTS // BLOCK // 2, last, 0)


def back(done, spots, own, away):
    return pl.pallas_call(
        back_kernel,
        name="back",
        in_specs=[VM] * 4,
        out_specs=VM,
        out_shape=jax.ShapeDtypeStruct((C, PTS), BF),
        scratch_shapes=[
            pltpu.VMEM((PTS, BLOCK), BF),
            pltpu.VMEM((PTS, BLOCK), BF),
            pltpu.VMEM((8, C, CAP), BF),
            pltpu.VMEM((C, 8 * CAP), BF),
            pltpu.SemaphoreType.DMA((8,)),
            pltpu.SemaphoreType.DMA((8,)),
        ],
        compiler_params=params(collective_id=2, has_side_effects=True),
    )(done, spots, own, away)


def on_device(
    feats, conv_weight, tap_index, halo_rows, hilbert_pos,
    ln1_gain, qkv_weight, out_weight, ln2_gain, mlp_in, mlp_out,
):
    feats_t = feats.T
    tap_t = tap_index.T
    halo, fetch, own, away, spot, groups, blank, cwt, qkvt, owt, g1, g2, w1t = halo_exchange(
        halo_rows[0], feats_t, hilbert_pos.reshape(32, 128), tap_t,
        conv_weight.reshape(TAPS * C, C), qkv_weight, out_weight,
        ln1_gain.reshape(1, C), ln2_gain.reshape(1, C), mlp_in,
    )
    updated, source = conv(
        groups, fetch.reshape(PTS), spot.reshape(CONV_STEPS, STEP, 128), tap_t, cwt, feats_t, halo,
        blank.reshape(SLOTS),
    )
    ordered, spots = deal(updated, source.reshape(SLOTS // 128, 128))
    done = windows(ordered, g1, qkvt, owt, g2, w1t, mlp_out.T)
    return back(done, spots, own, away).T


def solution(mesh):
    rows = P(("gx", "gy"), None)
    placed = (rows, P(), rows, P(("gx", "gy"), None, None), P(("gx", "gy"))) + (P(),) * 6
    return jax.shard_map(
        on_device, mesh=mesh, in_specs=placed, out_specs=rows, check_vma=False
    )
```

time: 201 us -> 193 us (0.960)
  Pallas kernels: 197 us -> 190 us
    pallas_call x1, Pallas kernels: 50.5 us -> 33.6 us  [conv(): pl.pallas_call(conv_kernel, name='conv', grid=(CONV_STEPS,), in_specs=[SM...]
    pallas_call x6 -> x4, Pallas kernels: 146 us -> 156 us  [the longest x1 60.8 us: windows(): pl.pallas_call(window_kernel, name='windows', in_specs=[VM] * 7, out_spec...]
    unnamed x0 -> x1, local copies, waits for them, and re-layouts: none -> 2.7 us
where the time goes in v2:
time: 193 us; the launch traced here: 192 us
  Pallas kernels  190 us (98%)
  local copies, waits for them, and re-layouts  2.7 us (1%)
    pallas_call x1, Pallas kernels, windows(): pl.pallas_call(window_kernel, name='windows', in_specs=[VM] * 7, out_spec...  60.8 us
    pallas_call x1, Pallas kernels, deal(): pl.pallas_call(deal_kernel, name='deal', in_specs=[VM, VM], out_specs=[VM...  37.6 us
    pallas_call x1, Pallas kernels, conv(): pl.pallas_call(conv_kernel, name='conv', grid=(CONV_STEPS,), in_specs=[SM...  33.6 us
    pallas_call x1, Pallas kernels, back(): pl.pallas_call(back_kernel, name='back', in_specs=[VM] * 4, out_specs=VM,...  28.9 us
    pallas_call x1, Pallas kernels, halo_exchange(): pl.pallas_call(halo_kernel, name='halo_exchange', in_specs=[VM] * 10, out...  28.6 us

profile of v2, /device:TPU:25, one launch (start us, length us, event | category | flops | bytes accessed | tf_op | source)
XLA Modules:
  0.0 192.3 jit_solution(5337258345865189271)
XLA Ops:
  0.0 28.6 %halo_exchange.1 = (bf16[8,192,512]{2,1,0:T(8,128)(2,1)}, s32[32,128]{1,0:T(8,128)}, s32[32,128]{1,0:T(8,128)}, s32[32,128]{1,0:T(8,128)}, s32[32,128]{1,0:T(8,1...) custom-call(s32[8,512]{1,0:T(8,128)} %bitcast.22, ...), custom_call_target="tpu_custom_call" | custom-call | tf_op jit(solution)/shard_map/halo_exchange/pallas_call | solution.py:216
  28.6 33.6 %conv.1 = (bf16[208,4096]{1,0:T(8,128)(2,1)}, s32[6144]{0:T(1024)}) custom-call(s32[27,128]{1,0:T(8,128)} %get-tuple-element.22.group_ref, s32[4096]{0:T(1024)} %bitcast.24, s32[8,4,128]{2,1,0:T(4,128)} %bitcast.25, s32[27,4096]{1,0:T(8,128)} %bitcast.18, bf16[192,5184]{1,0:T(8,128)(2,1)} %get-tuple-element.25.cwt_ref, bf16[192,4096]{1,0:T(8,128)(2,1)} %bitcast.15, ...), custom_call_target="tpu_custom_call" | custom-call | tf_op jit(solution)/shard_map/conv/pallas_call | solution.py:298
  62.2 37.6 %deal.1 = (bf16[192,4096]{1,0:T(8,128)(2,1)}, s32[8,256]{1,0:T(8,128)}) custom-call(bf16[208,4096]{1,0:T(8,128)(2,1)} %get-tuple-element.28.updated_ref, s32[48,128]{1,0:T(8,128)} %bitcast.21), custom_call_target="tpu_custom_call" | custom-call | tf_op jit(solution)/shard_map/deal/pallas_call | solution.py:402
  99.9 60.8 %windows.1.done_ref = bf16[192,4096]{1,0:T(8,128)(2,1)} custom-call(bf16[192,4096]{1,0:T(8,128)(2,1)} %get-tuple-element.30.in_ref, f32[192,128]{1,0:T(8,128)} %get-tuple-element.31.g1_ref, bf16[768,192]{1,0:T(8,128)(2,1)} %get-tuple-element.32.qkvt_ref, bf16[192,256]{1,0:T(8,128)(2,1)} %get-tuple-element.33.owt_ref, f32[192,128]{1,0:T(8,128)} %get-tuple-element.34.g2_ref, ...), custom_call_target="tpu_custom_call" | custom-call | tf_op jit(solution)/shard_map/windows/pallas_call | solution.py:490
  160.7 28.9 %back.1 = bf16[192,4096]{1,0:T(8,128)(2,1)} custom-call(bf16[192,4096]{1,0:T(8,128)(2,1)} %windows.1.done_ref, s32[8,256]{1,0:T(8,128)} %get-tuple-element.36.spots_ref, s32[32,128]{1,0:T(8,128)} %get-tuple-element.37.own_ref, s32[32,128]{1,0:T(8,128)} %get-tuple-element.38.away_ref), custom_call_target="tpu_custom_call" | custom-call | tf_op jit(solution)/shard_map/back/pallas_call | solution.py:584
  189.6 2.7 %copy.13 = bf16[4096,192]{0,1:T(8,128)(2,1)} copy(bf16[4096,192]{0,1:T(8,128)(2,1)} %bitcast.13) | data formatting | bytes 3145728

commit v3 on v2

--- a/solution.py
+++ b/solution.py
@@ -179,18 +179,14 @@
         select_columns(halo_ref[pl.ds(k, 1), :], onehot_a)
         select_columns(halo_ref[pl.ds(7 - k, 1), :], onehot_b)
 
-        @pl.when(i > 0)
-        def _():
-            start(7 - in_turn(i - 1))
-
         send[k] = jnp.dot(feats_ref[...], onehot_a[...], preferred_element_type=F32).astype(BF)
         send[7 - k] = jnp.dot(feats_ref[...], onehot_b[...], preferred_element_type=F32).astype(BF)
         start(k)
+        start(7 - k)
         return carry
 
     lax.fori_loop(0, 4, pair, 0)
     prepare_indices(hp_ref, tap_ref, fetch_ref, own_ref, away_ref, spot_ref, group_ref, blank_ref)
-    start(7 - in_turn(3))
     prepare_weights(
         cw_ref, qkvw_ref, ow_ref, g1_ref, g2_ref, w1_ref,
         cwt_ref, qkvt_ref, owt_ref, g1c_ref, g2c_ref, w1t_ref, pad,
@@ -345,23 +341,16 @@
         select_columns(index_row(source_ref, base + k * (CAP // 128), CAP // 128), first)
         select_columns(index_row(source_ref, base + (7 - k) * (CAP // 128), CAP // 128), second)
 
-        @pl.when(i > 0)
-        def _():
-            start(7 - in_turn(i - 1))
-
         send[k] = jnp.dot(updated_ref[...], first[...], preferred_element_type=F32).astype(BF)
         send[7 - k] = jnp.dot(updated_ref[...], second[...], preferred_element_type=F32).astype(BF)
         start(k)
+        start(7 - k)
         return carry
 
     lax.fori_loop(0, 4, pair, 0)
 
     def stay(n, carry):
         select_columns(index_row(source_ref, n * (BLOCK // 128), BLOCK // 128), onehot_a)
-
-        @pl.when(n == 0)
-        def _():
-            start(7 - in_turn(3))
 
         taken = jnp.dot(updated_ref[0:C, :], onehot_a[...], preferred_element_type=F32)
         out_ref[:, pl.ds(pl.multiple_of(n * BLOCK, BLOCK), BLOCK)] = taken.astype(BF)
@@ -464,7 +453,7 @@
                 attended[pl.ds(off, HP), :] = (mixed / mixed[HD : HD + 1, :]).astype(BF)
                 return inner
 
-            lax.fori_loop(0, HEADS, head, 0, unroll=1 if shifted else 2)
+            lax.fori_loop(0, HEADS, head, 0, unroll=1 if shifted else 4)
 
         @pl.when(safe)
         def _():
@@ -528,23 +517,16 @@
         select_columns(spots_ref[pl.ds(k, 1), :], first)
         select_columns(spots_ref[pl.ds(7 - k, 1), :], second)
 
-        @pl.when(i > 0)
-        def _():
-            start(7 - in_turn(i - 1))
-
         send[k] = jnp.dot(done_ref[...], first[...], preferred_element_type=F32).astype(BF)
         send[7 - k] = jnp.dot(done_ref[...], second[...], preferred_element_type=F32).astype(BF)
         start(k)
+        start(7 - k)
         return carry
 
     lax.fori_loop(0, 4, pair, 0)
 
     def stay(n, carry):
         select_columns(index_row(own_ref, n * (BLOCK // 128), BLOCK // 128), onehot_a)
-
-        @pl.when(n == 0)
-        def _():
-            start(7 - in_turn(3))
 
         taken = jnp.dot(done_ref[...], onehot_a[...], preferred_element_type=F32)
         out_ref[:, pl.ds(pl.multiple_of(n * BLOCK, BLOCK), BLOCK)] = taken.astype(BF)

time: 193 us -> 170 us (0.88)
  Pallas kernels: 190 us -> 167 us
    pallas_call x1, Pallas kernels: 28.9 us -> 20.2 us  [back(): pl.pallas_call(back_kernel, name='back', in_specs=[VM] * 4, out_specs=VM,...]
    pallas_call x1, Pallas kernels: 37.6 us -> 29.4 us  [deal(): pl.pallas_call(deal_kernel, name='deal', in_specs=[VM, VM], out_specs=[VM...]
    pallas_call x1, Pallas kernels: 28.6 us -> 23.2 us  [halo_exchange(): pl.pallas_call(halo_kernel, name='halo_exchange', in_specs=[VM] * 10, out...]
where the time goes in v3:
time: 170 us
  Pallas kernels  167 us (98%)
  local copies, waits for them, and re-layouts  2.7 us (2%)
    pallas_call x1, Pallas kernels, windows(): pl.pallas_call(window_kernel, name='windows', in_specs=[VM] * 7, out_spec...  60.8 us
    pallas_call x1, Pallas kernels, conv(): pl.pallas_call(conv_kernel, name='conv', grid=(CONV_STEPS,), in_specs=[SM...  33.6 us
    pallas_call x1, Pallas kernels, deal(): pl.pallas_call(deal_kernel, name='deal', in_specs=[VM, VM], out_specs=[VM...  29.4 us
    pallas_call x1, Pallas kernels, halo_exchange(): pl.pallas_call(halo_kernel, name='halo_exchange', in_specs=[VM] * 10, out...  23.2 us
    pallas_call x1, Pallas kernels, back(): pl.pallas_call(back_kernel, name='back', in_specs=[VM] * 4, out_specs=VM,...  20.2 us

profile of v3, /device:TPU:25, one launch (start us, length us, event | category | flops | bytes accessed | tf_op | source)
XLA Modules:
  0.0 170.0 jit_solution(2681627309146699688)
XLA Ops:
  0.0 23.2 %halo_exchange.1 = (bf16[8,192,512]{2,1,0:T(8,128)(2,1)}, s32[32,128]{1,0:T(8,128)}, s32[32,128]{1,0:T(8,128)}, s32[32,128]{1,0:T(8,128)}, s32[32,128]{1,0:T(8,1...) custom-call(s32[8,512]{1,0:T(8,128)} %bitcast.22, ...), custom_call_target="tpu_custom_call" | custom-call | tf_op jit(solution)/shard_map/halo_exchange/pallas_call | solution.py:212
  23.2 33.6 %conv.1 = (bf16[208,4096]{1,0:T(8,128)(2,1)}, s32[6144]{0:T(1024)}) custom-call(s32[27,128]{1,0:T(8,128)} %get-tuple-element.22.group_ref, s32[4096]{0:T(1024)} %bitcast.24, s32[8,4,128]{2,1,0:T(4,128)} %bitcast.25, s32[27,4096]{1,0:T(8,128)} %bitcast.18, bf16[192,5184]{1,0:T(8,128)(2,1)} %get-tuple-element.25.cwt_ref, bf16[192,4096]{1,0:T(8,128)(2,1)} %bitcast.15, ...), custom_call_target="tpu_custom_call" | custom-call | tf_op jit(solution)/shard_map/conv/pallas_call | solution.py:294
  56.8 29.4 %deal.1 = (bf16[192,4096]{1,0:T(8,128)(2,1)}, s32[8,256]{1,0:T(8,128)}) custom-call(bf16[208,4096]{1,0:T(8,128)(2,1)} %get-tuple-element.28.updated_ref, s32[48,128]{1,0:T(8,128)} %bitcast.21), custom_call_target="tpu_custom_call" | custom-call | tf_op jit(solution)/shard_map/deal/pallas_call | solution.py:391
  86.3 60.8 %windows.1.done_ref = bf16[192,4096]{1,0:T(8,128)(2,1)} custom-call(bf16[192,4096]{1,0:T(8,128)(2,1)} %get-tuple-element.30.in_ref, f32[192,128]{1,0:T(8,128)} %get-tuple-element.31.g1_ref, bf16[768,192]{1,0:T(8,128)(2,1)} %get-tuple-element.32.qkvt_ref, bf16[192,256]{1,0:T(8,128)(2,1)} %get-tuple-element.33.owt_ref, f32[192,128]{1,0:T(8,128)} %get-tuple-element.34.g2_ref, ...), custom_call_target="tpu_custom_call" | custom-call | tf_op jit(solution)/shard_map/windows/pallas_call | solution.py:479
  147.1 20.2 %back.1 = bf16[192,4096]{1,0:T(8,128)(2,1)} custom-call(bf16[192,4096]{1,0:T(8,128)(2,1)} %windows.1.done_ref, s32[8,256]{1,0:T(8,128)} %get-tuple-element.36.spots_ref, s32[32,128]{1,0:T(8,128)} %get-tuple-element.37.own_ref, s32[32,128]{1,0:T(8,128)} %get-tuple-element.38.away_ref), custom_call_target="tpu_custom_call" | custom-call | tf_op jit(solution)/shard_map/back/pallas_call | solution.py:566
  167.3 2.7 %copy.13 = bf16[4096,192]{0,1:T(8,128)(2,1)} copy(bf16[4096,192]{0,1:T(8,128)(2,1)} %bitcast.13) | data formatting | bytes 3145728

commit v4 on v3

--- a/solution.py
+++ b/solution.py
@@ -156,9 +156,17 @@
     halo_ref, feats_ref, hp_ref, tap_ref, cw_ref, qkvw_ref, ow_ref, g1_ref, g2_ref, w1_ref,
     out_ref, fetch_ref, own_ref, away_ref, spot_ref, group_ref, blank_ref,
     cwt_ref, qkvt_ref, owt_ref, g1c_ref, g2c_ref, w1t_ref,
-    onehot_a, onehot_b, send, zeros, pad, send_sem, recv_sem, zero_sem,
+    onehot, send, zeros, pad, cw, qkvw, ow, w1, tap, cwt, send_sem, recv_sem, zero_sem, load_sem,
 ):
     barrier, count = greet()
+    loads = [
+        pltpu.make_async_copy(src, dst, load_sem.at[i])
+        for i, (src, dst) in enumerate(
+            ((cw_ref, cw), (qkvw_ref, qkvw), (ow_ref, ow), (w1_ref, w1), (tap_ref, tap))
+        )
+    ]
+    for load in loads:
+        load.start()
     zeros[...] = jnp.zeros_like(zeros)
 
     def start(k):
@@ -174,23 +182,21 @@
 
     pl.semaphore_wait(barrier, count)
 
-    def pair(i, carry):
-        k = in_turn(i)
-        select_columns(halo_ref[pl.ds(k, 1), :], onehot_a)
-        select_columns(halo_ref[pl.ds(7 - k, 1), :], onehot_b)
-
-        send[k] = jnp.dot(feats_ref[...], onehot_a[...], preferred_element_type=F32).astype(BF)
-        send[7 - k] = jnp.dot(feats_ref[...], onehot_b[...], preferred_element_type=F32).astype(BF)
+    def one(i, carry):
+        pair = in_turn(i // 2)
+        k = jnp.where(i % 2 == 0, pair, 7 - pair)
+        select_columns(halo_ref[pl.ds(k, 1), :], onehot)
+        send[k] = jnp.dot(feats_ref[...], onehot[...], preferred_element_type=F32).astype(BF)
         start(k)
-        start(7 - k)
-        return carry
-
-    lax.fori_loop(0, 4, pair, 0)
-    prepare_indices(hp_ref, tap_ref, fetch_ref, own_ref, away_ref, spot_ref, group_ref, blank_ref)
-    prepare_weights(
-        cw_ref, qkvw_ref, ow_ref, g1_ref, g2_ref, w1_ref,
-        cwt_ref, qkvt_ref, owt_ref, g1c_ref, g2c_ref, w1t_ref, pad,
-    )
+        return carry
+
+    lax.fori_loop(0, 8, one, 0)
+    for load in loads:
+        load.wait()
+    prepare_weights(cw, qkvw, ow, g1_ref, g2_ref, w1, cwt, qkvt_ref, owt_ref, g1c_ref, g2c_ref, w1t_ref, pad)
+    store = pltpu.make_async_copy(cwt, cwt_ref, load_sem.at[5])
+    store.start()
+    prepare_indices(hp_ref, tap, fetch_ref, own_ref, away_ref, spot_ref, group_ref, blank_ref)
 
     def finish(k):
         inside = neighbour(k)[0]
@@ -205,6 +211,7 @@
             pltpu.make_async_copy(zeros, out_ref.at[k], zero_sem.at[k]).wait()
 
     each(finish)
+    store.wait()
 
 
 def halo_exchange(halo, feats_t, hp, tap_t, cw, qkvw, ow, g1, g2, w1):
@@ -212,8 +219,8 @@
     return pl.pallas_call(
         halo_kernel,
         name="halo_exchange",
-        in_specs=[VM] * 10,
-        out_specs=[ANY] + [VM] * 12,
+        in_specs=[VM, VM, VM, ANY, ANY, ANY, ANY, VM, VM, ANY],
+        out_specs=[ANY] + [VM] * 6 + [ANY] + [VM] * 5,
         out_shape=[
             sd((8, C, HB), BF),
             sd((32, 128), I32), sd((32, 128), I32), sd((32, 128), I32), sd((32, 128), I32),
@@ -223,70 +230,87 @@
         ],
         scratch_shapes=[
             pltpu.VMEM((PTS, HB), BF),
-            pltpu.VMEM((PTS, HB), BF),
             pltpu.VMEM((8, C, HB), BF),
             pltpu.VMEM((C, HB), BF),
             pltpu.VMEM((3 * HEADS * HP, C), F32),
+            pltpu.VMEM((TAPS * C, C), BF),
+            pltpu.VMEM((C, 3 * C), BF),
+            pltpu.VMEM((C, C), BF),
+            pltpu.VMEM((C, 4 * C), BF),
+            pltpu.VMEM((TAPS, PTS), I32),
+            pltpu.VMEM((C, TAPS * C), BF),
             pltpu.SemaphoreType.DMA((8,)),
             pltpu.SemaphoreType.DMA((8,)),
             pltpu.SemaphoreType.DMA((8,)),
+            pltpu.SemaphoreType.DMA((6,)),
         ],
         compiler_params=params(collective_id=0, has_side_effects=True),
     )(halo, feats_t, hp, tap_t, cw, qkvw, ow, g1, g2, w1)
 
 
-STEP = 4
-CONV_STEPS = PTS // (128 * STEP)
+STEP = 2
+PART = 128 * STEP
+PARTS = PTS // PART
+NOTES = -(-PART // (STEP * TAPS))
 
 
 def conv_kernel(
     group_ref, fetch_ref, spot_ref, tap_ref, cwt_ref, feats_ref, halo_ref, blank_ref,
-    out_ref, source_ref, lookup, gathered, load_sem,
+    out_ref, source_ref, lookup, even, odd, cwt, load_sem,
 ):
-    i = pl.program_id(0)
-
-    @pl.when(i == 0)
-    def _():
-        copies = [
-            pltpu.make_async_copy(blank_ref, source_ref, load_sem.at[9]),
-            pltpu.make_async_copy(feats_ref, lookup.at[:, 0:PTS], load_sem.at[8]),
-        ]
-        for k in range(8):
-            at = PTS + k * HB
-            copies.append(
-                pltpu.make_async_copy(halo_ref.at[k], lookup.at[:, at : at + HB], load_sem.at[k])
-            )
-        for copy in copies:
-            copy.start()
-        for copy in copies:
-            copy.wait()
-
-    for n in range(STEP):
-        def tap(t, carry):
-            start = pl.multiple_of(group_ref[t, i * STEP + n] * 128, 128)
-            source = lookup[:, pl.ds(start, 128)].astype(F32)
-            index = jnp.broadcast_to(tap_ref[pl.ds(t, 1), n * 128 : (n + 1) * 128], (C, 128))
-            taken = jnp.take_along_axis(source, index & 127, axis=1)
-            taken = jnp.where(index >= 0, taken, 0.0)
-            gathered[pl.ds(pl.multiple_of(t * C, C), C), n * 128 : (n + 1) * 128] = taken.astype(BF)
-            return carry
-
-        lax.fori_loop(0, TAPS, tap, 0, unroll=True)
-
-    def note(b, carry):
-        for u in range(32):
-            p = i * (128 * STEP) + b * 32 + u
-            source_ref[fetch_ref[p]] = p
-        return carry
-
-    lax.fori_loop(0, 4 * STEP, note, 0)
-    conv = jnp.dot(cwt_ref[...], gathered[...], preferred_element_type=F32)
-    here = lookup[:, pl.ds(pl.multiple_of(i * (128 * STEP), 128), 128 * STEP)].astype(F32)
-    out_ref[0:C, :] = (here + conv).astype(BF)
-    spot = index_row(spot_ref, 0, STEP) + 1
-    number = lax.broadcasted_iota(I32, (ROWS - C, 128 * STEP), 0)
-    digits = jnp.where(number == 0, spot // 64, jnp.where(number == 1, spot % 64, 0))
-    out_ref[C:ROWS, :] = digits.astype(F32).astype(BF)
+    weights = pltpu.make_async_copy(cwt_ref, cwt, load_sem.at[10])
+    copies = [
+        pltpu.make_async_copy(blank_ref, source_ref, load_sem.at[9]),
+        pltpu.make_async_copy(feats_ref, lookup.at[:, 0:PTS], load_sem.at[8]),
+    ]
+    for k in range(8):
+        at = PTS + k * HB
+        copies.append(
+            pltpu.make_async_copy(halo_ref.at[k], lookup.at[:, at : at + HB], load_sem.at[k])
+        )
+    for copy in copies:
+        copy.start()
+    weights.start()
+    for r in range(PTS // 128):
+        spot = spot_ref[r : r + 1, :] + 1
+        number = lax.broadcasted_iota(I32, (ROWS - C, 128), 0)
+        digits = jnp.where(number == 0, spot // 64, jnp.where(number == 1, spot % 64, 0))
+        out_ref[C:ROWS, r * 128 : (r + 1) * 128] = digits.astype(F32).astype(BF)
+    for copy in copies:
+        copy.wait()
+    weights.wait()
+
+    def gather(i, gathered):
+        for n in range(STEP):
+            for t in range(TAPS):
+                start = pl.multiple_of(group_ref[t, i * STEP + n] * 128, 128)
+                source = lookup[:, pl.ds(start, 128)].astype(F32)
+                lanes = pl.ds(pl.multiple_of(i * PART + n * 128, 128), 128)
+                index = jnp.broadcast_to(tap_ref[t : t + 1, lanes], (C, 128))
+                taken = jnp.take_along_axis(source, index & 127, axis=1)
+                taken = jnp.where(index >= 0, taken, 0.0)
+                gathered[t * C : (t + 1) * C, n * 128 : (n + 1) * 128] = taken.astype(BF)
+                first = (n * TAPS + t) * NOTES
+                points = [i * PART + u for u in range(first, min(first + NOTES, PART))]
+                places = [fetch_ref[p] for p in points]
+                for p, place in zip(points, places):
+                    source_ref[place] = p
+
+    def multiply(i, gathered):
+        at = pl.ds(pl.multiple_of(i * PART, PART), PART)
+        conv = jnp.dot(cwt[...], gathered[...], preferred_element_type=F32)
+        out_ref[0:C, at] = (lookup[:, at].astype(F32) + conv).astype(BF)
+
+    def two(j, carry):
+        multiply(jnp.maximum(2 * j - 1, 0), odd)
+        gather(2 * j, even)
+        multiply(2 * j, even)
+        gather(2 * j + 1, odd)
+        return carry
+
+    odd[...] = jnp.zeros_like(odd)
+    lax.fori_loop(0, PARTS // 2, two, 0)
+    multiply(PARTS - 1, odd)
 
 
 def conv(groups, fetch, spot, tap_t, cwt, feats_t, halo, blank):
@@ -294,22 +318,17 @@
     return pl.pallas_call(
         conv_kernel,
         name="conv",
-        grid=(CONV_STEPS,),
-        in_specs=[
-            SM, SM,
-            pl.BlockSpec((None, STEP, 128), lambda i: (i, 0, 0)),
-            pl.BlockSpec((TAPS, 128 * STEP), lambda i: (0, i)),
-            pl.BlockSpec((C, TAPS * C), lambda i: (0, 0), pipeline_mode=pl.Buffered(1)),
-            ANY, ANY, ANY,
-        ],
-        out_specs=[pl.BlockSpec((ROWS, 128 * STEP), lambda i: (0, i)), SM],
+        in_specs=[SM, SM, VM, VM, ANY, ANY, ANY, ANY],
+        out_specs=[VM, SM],
         out_shape=[sd((ROWS, PTS), BF), sd((SLOTS,), I32)],
         scratch_shapes=[
             pltpu.VMEM((C, PTS + 8 * HB), BF),
-            pltpu.VMEM((TAPS * C, 128 * STEP), BF),
-            pltpu.SemaphoreType.DMA((10,)),
+            pltpu.VMEM((TAPS * C, PART), BF),
+            pltpu.VMEM((TAPS * C, PART), BF),
+            pltpu.VMEM((C, TAPS * C), BF),
+            pltpu.SemaphoreType.DMA((11,)),
         ],
-        compiler_params=params(dimension_semantics=("arbitrary",)),
+        compiler_params=params(),
     )(groups, fetch, spot, tap_t, cwt, feats_t, halo, blank)
 
 
@@ -349,14 +368,15 @@
 
     lax.fori_loop(0, 4, pair, 0)
 
-    def stay(n, carry):
-        select_columns(index_row(source_ref, n * (BLOCK // 128), BLOCK // 128), onehot_a)
-
-        taken = jnp.dot(updated_ref[0:C, :], onehot_a[...], preferred_element_type=F32)
-        out_ref[:, pl.ds(pl.multiple_of(n * BLOCK, BLOCK), BLOCK)] = taken.astype(BF)
-        return carry
-
-    lax.fori_loop(0, PTS // BLOCK, stay, 0)
+    def stay(m, carry):
+        for n, onehot in ((2 * m, onehot_a), (2 * m + 1, onehot_b)):
+            select_columns(index_row(source_ref, n * (BLOCK // 128), BLOCK // 128), onehot)
+        for n, onehot in ((2 * m, onehot_a), (2 * m + 1, onehot_b)):
+            taken = jnp.dot(updated_ref[0:C, :], onehot[...], preferred_element_type=F32)
+            out_ref[:, pl.ds(pl.multiple_of(n * BLOCK, BLOCK), BLOCK)] = taken.astype(BF)
+        return carry
+
+    lax.fori_loop(0, PTS // BLOCK // 2, stay, 0)
 
     def finish(k):
         @pl.when(neighbour(k)[0])
@@ -490,7 +510,7 @@
     )(ordered, g1, qkvt, owt, g2, w1t, w2t)
 
 
-def back_kernel(done_ref, spots_ref, own_ref, away_ref, out_ref, onehot_a, onehot_b, send, recv, send_sem, recv_sem):
+def back_kernel(done_ref, spots_ref, own_ref, out_ref, recv, onehot_a, onehot_b, send, send_sem, recv_sem):
     barrier, count = greet()
 
     def landing(k):
@@ -525,14 +545,15 @@
 
     lax.fori_loop(0, 4, pair, 0)
 
-    def stay(n, carry):
-        select_columns(index_row(own_ref, n * (BLOCK // 128), BLOCK // 128), onehot_a)
-
-        taken = jnp.dot(done_ref[...], onehot_a[...], preferred_element_type=F32)
-        out_ref[:, pl.ds(pl.multiple_of(n * BLOCK, BLOCK), BLOCK)] = taken.astype(BF)
-        return carry
-
-    lax.fori_loop(0, PTS // BLOCK, stay, 0)
+    def stay(m, carry):
+        for n, onehot in ((2 * m, onehot_a), (2 * m + 1, onehot_b)):
+            select_columns(index_row(own_ref, n * (BLOCK // 128), BLOCK // 128), onehot)
+        for n, onehot in ((2 * m, onehot_a), (2 * m + 1, onehot_b)):
+            taken = jnp.dot(done_ref[...], onehot[...], preferred_element_type=F32)
+            out_ref[:, pl.ds(pl.multiple_of(n * BLOCK, BLOCK), BLOCK)] = taken.astype(BF)
+        return carry
+
+    lax.fori_loop(0, PTS // BLOCK // 2, stay, 0)
 
     def finish(k):
         @pl.when(neighbour(k)[0])
@@ -541,44 +562,57 @@
             push(7 - k, send.at[k], landing(k), send_sem, recv_sem).wait_recv()
 
     each(finish)
-    depth = 8 * CAP
-
-    def returned(n, onehot):
-        select_columns(index_row(away_ref, n * (BLOCK // 128), BLOCK // 128), onehot.at[0:depth, :])
-
-    def add(n, onehot):
-        taken = jnp.dot(recv[...], onehot[0:depth, :], preferred_element_type=F32)
-        at = pl.multiple_of(n * BLOCK, BLOCK)
-        here = out_ref[:, pl.ds(at, BLOCK)].astype(F32) + taken
-        out_ref[:, pl.ds(at, BLOCK)] = here.astype(BF)
-
-    def last(m, carry):
-        returned(2 * m, onehot_a)
-        returned(2 * m + 1, onehot_b)
-        add(2 * m, onehot_a)
-        add(2 * m + 1, onehot_b)
-        return carry
-
-    lax.fori_loop(0, PTS // BLOCK // 2, last, 0)
-
-
-def back(done, spots, own, away):
+
+
+def back(done, spots, own):
+    sd = jax.ShapeDtypeStruct
     return pl.pallas_call(
         back_kernel,
         name="back",
-        in_specs=[VM] * 4,
-        out_specs=VM,
-        out_shape=jax.ShapeDtypeStruct((C, PTS), BF),
+        in_specs=[VM] * 3,
+        out_specs=[VM, VM],
+        out_shape=[sd((C, PTS), BF), sd((C, 8 * CAP), BF)],
         scratch_shapes=[
             pltpu.VMEM((PTS, BLOCK), BF),
             pltpu.VMEM((PTS, BLOCK), BF),
             pltpu.VMEM((8, C, CAP), BF),
-            pltpu.VMEM((C, 8 * CAP), BF),
             pltpu.SemaphoreType.DMA((8,)),
             pltpu.SemaphoreType.DMA((8,)),
         ],
         compiler_params=params(collective_id=2, has_side_effects=True),
-    )(done, spots, own, away)
+    )(done, spots, own)
+
+
+WIDE = 1024
+
+
+def collect_kernel(kept_ref, returned_ref, away_ref, out_ref, onehot_a, onehot_b):
+    i = pl.program_id(0)
+    halves = ((0, onehot_a), (BLOCK, onehot_b))
+    for at, onehot in halves:
+        first = i * (WIDE // 128) + at // 128
+        select_columns(index_row(away_ref, first, BLOCK // 128), onehot)
+    for at, onehot in halves:
+        taken = jnp.dot(returned_ref[...], onehot[...], preferred_element_type=F32)
+        kept = kept_ref[:, at : at + BLOCK].astype(F32)
+        out_ref[:, at : at + BLOCK] = (kept + taken).astype(BF)
+
+
+def collect(kept, returned, away):
+    return pl.pallas_call(
+        collect_kernel,
+        name="collect",
+        grid=(PTS // WIDE,),
+        in_specs=[
+            pl.BlockSpec((C, WIDE), lambda i: (0, i)),
+            pl.BlockSpec((C, 8 * CAP), lambda i: (0, 0)),
+            pl.BlockSpec((32, 128), lambda i: (0, 0)),
+        ],
+        out_specs=pl.BlockSpec((C, WIDE), lambda i: (0, i)),
+        out_shape=jax.ShapeDtypeStruct((C, PTS), BF),
+        scratch_shapes=[pltpu.VMEM((8 * CAP, BLOCK), BF), pltpu.VMEM((8 * CAP, BLOCK), BF)],
+        compiler_params=params(dimension_semantics=("arbitrary",)),
+    )(kept, returned, away)
 
 
 def on_device(
@@ -593,12 +627,13 @@
         ln1_gain.reshape(1, C), ln2_gain.reshape(1, C), mlp_in,
     )
     updated, source = conv(
-        groups, fetch.reshape(PTS), spot.reshape(CONV_STEPS, STEP, 128), tap_t, cwt, feats_t, halo,
+        groups, fetch.reshape(PTS), spot, tap_t, cwt, feats_t, halo,
         blank.reshape(SLOTS),
     )
     ordered, spots = deal(updated, source.reshape(SLOTS // 128, 128))
     done = windows(ordered, g1, qkvt, owt, g2, w1t, mlp_out.T)
-    return back(done, spots, own, away).T
+    kept, returned = back(done, spots, own)
+    return collect(kept, returned, away).T
 
 
 def solution(mesh):

time: 170 us -> 160 us (0.941)
  Pallas kernels: 167 us -> 159 us
  local copies, waits for them, and re-layouts: 2.7 us -> 0 us
    pallas_call x3 -> x4, Pallas kernels: 77 us -> 70.6 us  [the longest x1 26.3 us: conv(): pl.pallas_call(conv_kernel, name='conv', in_specs=[SM, SM, VM, VM, ANY, A...]
    unnamed x1 -> x0, local copies, waits for them, and re-layouts: 2.7 us -> none
where the time goes in v4:
time: 160 us; the launch traced here: 159 us
  Pallas kernels  159 us (99%)
    pallas_call x1, Pallas kernels, windows(): pl.pallas_call(window_kernel, name='windows', in_specs=[VM] * 7, out_spec...  60.8 us
    pallas_call x1, Pallas kernels, deal(): pl.pallas_call(deal_kernel, name='deal', in_specs=[VM, VM], out_specs=[VM...  27.8 us
    pallas_call x1, Pallas kernels, conv(): pl.pallas_call(conv_kernel, name='conv', in_specs=[SM, SM, VM, VM, ANY, A...  26.3 us
    pallas_call x1, Pallas kernels, halo_exchange(): pl.pallas_call(halo_kernel, name='halo_exchange', in_specs=[VM, VM, VM, A...  21.5 us
    pallas_call x1, Pallas kernels, back(): pl.pallas_call(back_kernel, name='back', in_specs=[VM] * 3, out_specs=[VM...  16.5 us
    pallas_call x1, Pallas kernels, collect(): pl.pallas_call(collect_kernel, name='collect', grid=(PTS // WIDE,), in_sp...  6.22 us

profile of v4, /device:TPU:25, one launch (start us, length us, event | category | flops | bytes accessed | tf_op | source)
XLA Modules:
  0.0 159.3 jit_solution(361829131251379561)
XLA Ops:
  0.0 21.5 %halo_exchange.1 = (bf16[8,192,512]{2,1,0:T(8,128)(2,1)}, s32[32,128]{1,0:T(8,128)}, s32[32,128]{1,0:T(8,128)}, s32[32,128]{1,0:T(8,128)}, s32[32,128]{1,0:T(8,1...) custom-call(s32[8,512]{1,0:T(8,128)} %bitcast.20, ...), custom_call_target="tpu_custom_call" | custom-call | tf_op jit(solution)/shard_map/halo_exchange/pallas_call | solution.py:219
  21.6 26.3 %conv.1 = (bf16[208,4096]{1,0:T(8,128)(2,1)}, s32[6144]{0:T(1024)}) custom-call(s32[27,128]{1,0:T(8,128)} %get-tuple-element.24.group_ref, s32[4096]{0:T(1024)} %bitcast.22, s32[32,128]{1,0:T(8,128)} %get-tuple-element.26.spot_ref, s32[27,4096]{1,0:T(8,128)} %bitcast.16, bf16[192,5184]{1,0:T(8,128)(2,1)} %get-tuple-element.27.cwt_ref, ...), custom_call_target="tpu_custom_call" | custom-call | tf_op jit(solution)/shard_map/conv/pallas_call | solution.py:318
  47.9 27.8 %deal.1 = (bf16[192,4096]{1,0:T(8,128)(2,1)}, s32[8,256]{1,0:T(8,128)}) custom-call(bf16[208,4096]{1,0:T(8,128)(2,1)} %get-tuple-element.30.updated_ref, s32[48,128]{1,0:T(8,128)} %bitcast.19), custom_call_target="tpu_custom_call" | custom-call | tf_op jit(solution)/shard_map/deal/pallas_call | solution.py:411
  75.7 60.8 %windows.1.done_ref = bf16[192,4096]{1,0:T(8,128)(2,1)} custom-call(bf16[192,4096]{1,0:T(8,128)(2,1)} %get-tuple-element.32.in_ref, f32[192,128]{1,0:T(8,128)} %get-tuple-element.33.g1_ref, bf16[768,192]{1,0:T(8,128)(2,1)} %get-tuple-element.34.qkvt_ref, bf16[192,256]{1,0:T(8,128)(2,1)} %get-tuple-element.35.owt_ref, f32[192,128]{1,0:T(8,128)} %get-tuple-element.36.g2_ref, ...), custom_call_target="tpu_custom_call" | custom-call | tf_op jit(solution)/shard_map/windows/pallas_call | solution.py:499
  136.6 16.5 %back.1 = (bf16[192,4096]{1,0:T(8,128)(2,1)}, bf16[192,2048]{1,0:T(8,128)(2,1)}) custom-call(bf16[192,4096]{1,0:T(8,128)(2,1)} %windows.1.done_ref, s32[8,256]{1,0:T(8,128)} %get-tuple-element.38.spots_ref, s32[32,128]{1,0:T(8,128)} %get-tuple-element.39.own_ref), custom_call_target="tpu_custom_call" | custom-call | tf_op jit(solution)/shard_map/back/pallas_call | solution.py:569
  153.1 6.2 %collect.1 = bf16[192,4096]{1,0:T(8,128)(2,1)} custom-call(bf16[192,4096]{1,0:T(8,128)(2,1)} %get-tuple-element.40.kept_ref, bf16[192,2048]{1,0:T(8,128)(2,1)} %get-tuple-element.41.returned_ref, s32[32,128]{1,0:T(8,128)} %get-tuple-element.42.away_ref), custom_call_target="tpu_custom_call" | custom-call | tf_op jit(solution)/shard_map/collect/pallas_call | solution.py:602

commit v5 on v4

--- a/solution.py
+++ b/solution.py
@@ -23,7 +23,6 @@
 HB = 512
 CAP = PTS // 16
 GROUP = 128
-SLOTS = PTS + 8 * CAP
 ROWS = C + 16
 VMEM_LIMIT = 60 * 1024 * 1024
 SCALE = 1.0 / math.sqrt(HD) * math.log2(math.e)
@@ -92,7 +91,22 @@
         onehot[s : s + 256, :] = jnp.where(place == index, 1.0, 0.0).astype(BF)
 
 
-def prepare_indices(hp_ref, tap_ref, fetch_ref, own_ref, away_ref, spot_ref, group_ref, blank_ref):
+def spread_index(row):
+    return jnp.broadcast_to(row, (128, row.shape[1])).T
+
+
+def place_rows(index, base, onehot):
+    depth, width = onehot.shape
+    for s in range(0, depth, 256):
+        here = index[s : s + 256, :] - base
+        hits = [
+            jnp.where(lax.broadcasted_iota(I32, (256, 128), 1) + d == here, 1.0, 0.0)
+            for d in range(0, width, 128)
+        ]
+        onehot[s : s + 256, :] = jnp.concatenate(hits, 1).astype(BF)
+
+
+def prepare_indices(hp_ref, tap_ref, fetch_ref, own_ref, away_ref, spot_ref, group_ref):
     ix = lax.axis_index("gx")
     iy = lax.axis_index("gy")
     ny = lax.axis_size("gy")
@@ -123,7 +137,6 @@
     own_ref[...] = jnp.where(own, local, -1)
     away_ref[...] = jnp.where(own, -1, away)
     spot_ref[...] = local
-    blank_ref[...] = jnp.full_like(blank_ref, -1)
     lane = lax.broadcasted_iota(I32, (TAPS, 128), 1)
     groups = jnp.zeros((TAPS, 128), I32)
     for i in range(PTS // 128):
@@ -154,7 +167,7 @@
 
 def halo_kernel(
     halo_ref, feats_ref, hp_ref, tap_ref, cw_ref, qkvw_ref, ow_ref, g1_ref, g2_ref, w1_ref,
-    out_ref, fetch_ref, own_ref, away_ref, spot_ref, group_ref, blank_ref,
+    out_ref, fetch_ref, own_ref, away_ref, spot_ref, group_ref,
     cwt_ref, qkvt_ref, owt_ref, g1c_ref, g2c_ref, w1t_ref,
     onehot, send, zeros, pad, cw, qkvw, ow, w1, tap, cwt, send_sem, recv_sem, zero_sem, load_sem,
 ):
@@ -196,7 +209,7 @@
     prepare_weights(cw, qkvw, ow, g1_ref, g2_ref, w1, cwt, qkvt_ref, owt_ref, g1c_ref, g2c_ref, w1t_ref, pad)
     store = pltpu.make_async_copy(cwt, cwt_ref, load_sem.at[5])
     store.start()
-    prepare_indices(hp_ref, tap, fetch_ref, own_ref, away_ref, spot_ref, group_ref, blank_ref)
+    prepare_indices(hp_ref, tap, fetch_ref, own_ref, away_ref, spot_ref, group_ref)
 
     def finish(k):
         inside = neighbour(k)[0]
@@ -220,11 +233,11 @@
         halo_kernel,
         name="halo_exchange",
         in_specs=[VM, VM, VM, ANY, ANY, ANY, ANY, VM, VM, ANY],
-        out_specs=[ANY] + [VM] * 6 + [ANY] + [VM] * 5,
+        out_specs=[ANY] + [VM] * 5 + [ANY] + [VM] * 5,
         out_shape=[
             sd((8, C, HB), BF),
             sd((32, 128), I32), sd((32, 128), I32), sd((32, 128), I32), sd((32, 128), I32),
-            sd((TAPS, 128), I32), sd((SLOTS // 128, 128), I32),
+            sd((TAPS, 128), I32),
             sd((C, TAPS * C), BF), sd((3 * HEADS * HP, C), BF), sd((C, HEADS * HP), BF),
             sd((C, 128), F32), sd((C, 128), F32), sd((4 * C, C), BF),
         ],
@@ -251,16 +264,13 @@
 STEP = 2
 PART = 128 * STEP
 PARTS = PTS // PART
-NOTES = -(-PART // (STEP * TAPS))
 
 
 def conv_kernel(
-    group_ref, fetch_ref, spot_ref, tap_ref, cwt_ref, feats_ref, halo_ref, blank_ref,
-    out_ref, source_ref, lookup, even, odd, cwt, load_sem,
+    group_ref, spot_ref, tap_ref, cwt_ref, feats_ref, halo_ref, out_ref, lookup, even, odd, cwt, load_sem,
 ):
-    weights = pltpu.make_async_copy(cwt_ref, cwt, load_sem.at[10])
+    weights = pltpu.make_async_copy(cwt_ref, cwt, load_sem.at[9])
     copies = [
-        pltpu.make_async_copy(blank_ref, source_ref, load_sem.at[9]),
         pltpu.make_async_copy(feats_ref, lookup.at[:, 0:PTS], load_sem.at[8]),
     ]
     for k in range(8):
@@ -290,11 +300,6 @@
                 taken = jnp.take_along_axis(source, index & 127, axis=1)
                 taken = jnp.where(index >= 0, taken, 0.0)
                 gathered[t * C : (t + 1) * C, n * 128 : (n + 1) * 128] = taken.astype(BF)
-                first = (n * TAPS + t) * NOTES
-                points = [i * PART + u for u in range(first, min(first + NOTES, PART))]
-                places = [fetch_ref[p] for p in points]
-                for p, place in zip(points, places):
-                    source_ref[place] = p
 
     def multiply(i, gathered):
         at = pl.ds(pl.multiple_of(i * PART, PART), PART)
@@ -313,52 +318,57 @@
     multiply(PARTS - 1, odd)
 
 
-def conv(groups, fetch, spot, tap_t, cwt, feats_t, halo, blank):
-    sd = jax.ShapeDtypeStruct
+def conv(groups, spot, tap_t, cwt, feats_t, halo):
     return pl.pallas_call(
         conv_kernel,
         name="conv",
-        in_specs=[SM, SM, VM, VM, ANY, ANY, ANY, ANY],
-        out_specs=[VM, SM],
-        out_shape=[sd((ROWS, PTS), BF), sd((SLOTS,), I32)],
+        in_specs=[SM, VM, VM, ANY, ANY, ANY],
+        out_specs=VM,
+        out_shape=jax.ShapeDtypeStruct((ROWS, PTS), BF),
         scratch_shapes=[
             pltpu.VMEM((C, PTS + 8 * HB), BF),
             pltpu.VMEM((TAPS * C, PART), BF),
             pltpu.VMEM((TAPS * C, PART), BF),
             pltpu.VMEM((C, TAPS * C), BF),
-            pltpu.SemaphoreType.DMA((11,)),
+            pltpu.SemaphoreType.DMA((10,)),
         ],
         compiler_params=params(),
-    )(groups, fetch, spot, tap_t, cwt, feats_t, halo, blank)
+    )(groups, spot, tap_t, cwt, feats_t, halo)
 
 
 BLOCK = 512
 
 
-def deal_kernel(updated_ref, source_ref, out_ref, spots_ref, onehot_a, onehot_b, send, recv, send_sem, recv_sem):
+def deal_kernel(
+    updated_ref, fetch_ref, out_ref, spots_ref, index, onehot_a, onehot_b, send, recv, send_sem, recv_sem
+):
     barrier, count = greet()
+
+    def landing(k):
+        return recv.at[:, pl.ds(pl.multiple_of(k * CAP, CAP), CAP)]
 
     def blank(k):
         @pl.when(jnp.logical_not(neighbour(k)[0]))
         def _():
-            recv[k] = jnp.zeros((ROWS, CAP), BF)
+            recv[:, pl.ds(pl.multiple_of(k * CAP, CAP), CAP)] = jnp.zeros((ROWS, CAP), BF)
 
     each(blank)
 
     def start(k):
         @pl.when(neighbour(k)[0])
         def _():
-            push(k, send.at[k], recv.at[7 - k], send_sem, recv_sem).start()
-
+            push(k, send.at[k], landing(7 - k), send_sem, recv_sem).start()
+
+    for r in range(PTS // 128):
+        index[r * 128 : (r + 1) * 128, :] = spread_index(fetch_ref[r : r + 1, :])
     pl.semaphore_wait(barrier, count)
     first = onehot_a.at[:, 0:CAP]
     second = onehot_b.at[:, 0:CAP]
 
     def pair(i, carry):
         k = in_turn(i)
-        base = PTS // 128
-        select_columns(index_row(source_ref, base + k * (CAP // 128), CAP // 128), first)
-        select_columns(index_row(source_ref, base + (7 - k) * (CAP // 128), CAP // 128), second)
+        place_rows(index, PTS + k * CAP, first)
+        place_rows(index, PTS + (7 - k) * CAP, second)
 
         send[k] = jnp.dot(updated_ref[...], first[...], preferred_element_type=F32).astype(BF)
         send[7 - k] = jnp.dot(updated_ref[...], second[...], preferred_element_type=F32).astype(BF)
@@ -370,7 +380,7 @@
 
     def stay(m, carry):
         for n, onehot in ((2 * m, onehot_a), (2 * m + 1, onehot_b)):
-            select_columns(index_row(source_ref, n * (BLOCK // 128), BLOCK // 128), onehot)
+            place_rows(index, n * BLOCK, onehot)
         for n, onehot in ((2 * m, onehot_a), (2 * m + 1, onehot_b)):
             taken = jnp.dot(updated_ref[0:C, :], onehot[...], preferred_element_type=F32)
             out_ref[:, pl.ds(pl.multiple_of(n * BLOCK, BLOCK), BLOCK)] = taken.astype(BF)
@@ -381,32 +391,34 @@
     def finish(k):
         @pl.when(neighbour(k)[0])
         def _():
-            push(k, send.at[k], recv.at[7 - k], send_sem, recv_sem).wait_send()
-            push(7 - k, send.at[k], recv.at[k], send_sem, recv_sem).wait_recv()
+            push(k, send.at[k], landing(7 - k), send_sem, recv_sem).wait_send()
+            push(7 - k, send.at[k], landing(k), send_sem, recv_sem).wait_recv()
 
     each(finish)
 
+    depth = 8 * CAP
     for k in range(8):
-        digits = recv[k, C:ROWS, :].astype(F32)
-        spots_ref[k : k + 1, :] = (digits[0:1, :] * 64.0 + digits[1:2, :] - 1.0).astype(I32)
-
-    def arrive(n, carry):
-        total = jnp.zeros((C, BLOCK), F32)
-        at = pl.multiple_of(n * BLOCK, BLOCK)
-        place = lax.broadcasted_iota(I32, (BLOCK, CAP), 0) + at
-        for k in range(8):
-            chosen = jnp.where(place == spots_ref[k : k + 1, :], 1.0, 0.0).astype(BF)
-            total = total + lax.dot_general(
-                recv[k, 0:C, :], chosen, (((1,), (1,)), ((), ())), preferred_element_type=F32
-            )
-        here = out_ref[:, pl.ds(at, BLOCK)].astype(F32) + total
-        out_ref[:, pl.ds(at, BLOCK)] = here.astype(BF)
-        return carry
-
-    lax.fori_loop(0, PTS // BLOCK, arrive, 0)
-
-
-def deal(updated, source):
+        digits = recv[C:ROWS, k * CAP : (k + 1) * CAP].astype(F32)
+        spot = (digits[0:1, :] * 64.0 + digits[1:2, :] - 1.0).astype(I32)
+        spots_ref[k : k + 1, :] = spot
+        for c in range(0, CAP, 128):
+            at = k * CAP + c
+            index[at : at + 128, :] = spread_index(spot[:, c : c + 128])
+
+    def arrive(m, carry):
+        blocks = ((2 * m, onehot_a), (2 * m + 1, onehot_b))
+        for n, onehot in blocks:
+            place_rows(index, n * BLOCK, onehot.at[0:depth, :])
+        for n, onehot in blocks:
+            at = pl.ds(pl.multiple_of(n * BLOCK, BLOCK), BLOCK)
+            taken = jnp.dot(recv[0:C, :], onehot[0:depth, :], preferred_element_type=F32)
+            out_ref[:, at] = (out_ref[:, at].astype(F32) + taken).astype(BF)
+        return carry
+
+    lax.fori_loop(0, PTS // BLOCK // 2, arrive, 0)
+
+
+def deal(updated, fetch):
     sd = jax.ShapeDtypeStruct
     return pl.pallas_call(
         deal_kernel,
@@ -415,15 +427,16 @@
         out_specs=[VM, VM],
         out_shape=[sd((C, PTS), BF), sd((8, CAP), I32)],
         scratch_shapes=[
+            pltpu.VMEM((PTS, 128), I32),
             pltpu.VMEM((PTS, BLOCK), BF),
             pltpu.VMEM((PTS, BLOCK), BF),
             pltpu.VMEM((8, ROWS, CAP), BF),
-            pltpu.VMEM((8, ROWS, CAP), BF),
+            pltpu.VMEM((ROWS, 8 * CAP), BF),
             pltpu.SemaphoreType.DMA((8,)),
             pltpu.SemaphoreType.DMA((8,)),
         ],
         compiler_params=params(collective_id=1, has_side_effects=True),
-    )(updated, source)
+    )(updated, fetch)
 
 
 def norm_columns(values, gain):
@@ -436,77 +449,73 @@
 def window_kernel(
     in_ref, g1_ref, qkvt_ref, owt_ref, g2_ref, w1t_ref, w2t_ref, out_ref, packed, attended
 ):
-    def window(w, carry):
-        base = pl.multiple_of(w * WIN, WIN)
-        x = in_ref[:, pl.ds(base, WIN)].astype(F32)
-        normed = norm_columns(x, g1_ref[:, 0:1])
-        wide = HEADS * HP
-        queries = jnp.dot(qkvt_ref[0:wide, :], normed, preferred_element_type=F32) * SCALE
-        packed[0:wide, :] = queries.astype(BF)
-        packed[wide : 3 * wide, :] = jnp.dot(
-            qkvt_ref[wide : 3 * wide, :], normed, preferred_element_type=F32
-        ).astype(BF)
-        largest_q = jnp.zeros((1, WIN), F32)
-        largest_k = jnp.zeros((1, WIN), F32)
-        for h in range(HEADS):
-            q = packed[h * HP : (h + 1) * HP, :].astype(F32)
-            key = packed[wide + h * HP : wide + (h + 1) * HP, :].astype(F32)
-            largest_q = jnp.maximum(largest_q, jnp.sum(q * q, 0, keepdims=True))
-            largest_k = jnp.maximum(largest_k, jnp.sum(key * key, 0, keepdims=True))
-        safe = jnp.max(largest_q) * jnp.max(largest_k) <= SAFE * SAFE
-
-        def heads(shifted):
-            def head(h, inner):
-                off = pl.multiple_of(h * HP, HP)
-                q = packed[pl.ds(off, HP), :]
-                key = packed[pl.ds(wide + off, HP), :]
-                value = packed[pl.ds(2 * wide + off, HP), :]
-                number = lax.broadcasted_iota(I32, (HP, WIN), 0)
-                value = jnp.where(number == HD, jnp.ones_like(value), value)
-                scores = lax.dot_general(
-                    key, q, (((0,), (0,)), ((), ())), preferred_element_type=F32
-                )
-                if shifted:
-                    scores = scores - jnp.max(scores, 0, keepdims=True)
-                probs = jnp.exp2(scores).astype(BF)
-                mixed = jnp.dot(value, probs, preferred_element_type=F32)
-                attended[pl.ds(off, HP), :] = (mixed / mixed[HD : HD + 1, :]).astype(BF)
-                return inner
-
-            lax.fori_loop(0, HEADS, head, 0, unroll=1 if shifted else 4)
-
-        @pl.when(safe)
-        def _():
-            heads(False)
-
-        @pl.when(jnp.logical_not(safe))
-        def _():
-            heads(True)
-
-        residual = x + jnp.dot(owt_ref[...], attended[...], preferred_element_type=F32)
-        residual = residual.astype(BF).astype(F32)
-        normed_two = norm_columns(residual, g2_ref[:, 0:1])
-        hidden = jnp.dot(w1t_ref[...], normed_two, preferred_element_type=F32)
-        hidden = 0.5 * hidden * (1.0 + lax.erf(hidden * (2.0**-0.5)))
-        processed = residual + jnp.dot(w2t_ref[...], hidden.astype(BF), preferred_element_type=F32)
-        out_ref[:, pl.ds(base, WIN)] = processed.astype(BF)
-        return carry
-
-    lax.fori_loop(0, PTS // WIN, window, 0)
+    x = in_ref[...].astype(F32)
+    normed = norm_columns(x, g1_ref[:, 0:1])
+    wide = HEADS * HP
+    queries = jnp.dot(qkvt_ref[0:wide, :], normed, preferred_element_type=F32) * SCALE
+    packed[0:wide, :] = queries.astype(BF)
+    packed[wide : 3 * wide, :] = jnp.dot(
+        qkvt_ref[wide : 3 * wide, :], normed, preferred_element_type=F32
+    ).astype(BF)
+    largest_q = jnp.zeros((1, WIN), F32)
+    largest_k = jnp.zeros((1, WIN), F32)
+    for h in range(HEADS):
+        q = packed[h * HP : (h + 1) * HP, :].astype(F32)
+        key = packed[wide + h * HP : wide + (h + 1) * HP, :].astype(F32)
+        largest_q = jnp.maximum(largest_q, jnp.sum(q * q, 0, keepdims=True))
+        largest_k = jnp.maximum(largest_k, jnp.sum(key * key, 0, keepdims=True))
+    safe = jnp.max(largest_q) * jnp.max(largest_k) <= SAFE * SAFE
+
+    def heads(shifted):
+        def head(h, inner):
+            off = pl.multiple_of(h * HP, HP)
+            q = packed[pl.ds(off, HP), :]
+            key = packed[pl.ds(wide + off, HP), :]
+            value = packed[pl.ds(2 * wide + off, HP), :]
+            number = lax.broadcasted_iota(I32, (HP, WIN), 0)
+            value = jnp.where(number == HD, jnp.ones_like(value), value)
+            scores = lax.dot_general(
+                key, q, (((0,), (0,)), ((), ())), preferred_element_type=F32
+            )
+            if shifted:
+                scores = scores - jnp.max(scores, 0, keepdims=True)
+            probs = jnp.exp2(scores).astype(BF)
+            mixed = jnp.dot(value, probs, preferred_element_type=F32)
+            attended[pl.ds(off, HP), :] = (mixed / mixed[HD : HD + 1, :]).astype(BF)
+            return inner
+
+        lax.fori_loop(0, HEADS, head, 0, unroll=1 if shifted else 8)
+
+    @pl.when(safe)
+    def _():
+        heads(False)
+
+    @pl.when(jnp.logical_not(safe))
+    def _():
+        heads(True)
+
+    residual = x + jnp.dot(owt_ref[...], attended[...], preferred_element_type=F32)
+    residual = residual.astype(BF).astype(F32)
+    normed_two = norm_columns(residual, g2_ref[:, 0:1])
+    hidden = jnp.dot(w1t_ref[...], normed_two, preferred_element_type=F32)
+    hidden = 0.5 * hidden * (1.0 + lax.erf(hidden * (2.0**-0.5)))
+    processed = residual + jnp.dot(w2t_ref[...], hidden.astype(BF), preferred_element_type=F32)
+    out_ref[...] = processed.astype(BF)
 
 
 def windows(ordered, g1, qkvt, owt, g2, w1t, w2t):
     return pl.pallas_call(
         window_kernel,
         name="windows",
-        in_specs=[VM] * 7,
-        out_specs=VM,
+        grid=(PTS // WIN,),
+        in_specs=[pl.BlockSpec((C, WIN), lambda i: (0, i)), VM, VM, VM, VM, VM, VM],
+        out_specs=pl.BlockSpec((C, WIN), lambda i: (0, i)),
         out_shape=jax.ShapeDtypeStruct((C, PTS), BF),
         scratch_shapes=[
             pltpu.VMEM((3 * HEADS * HP, WIN), BF),
             pltpu.VMEM((HEADS * HP, WIN), BF),
         ],
-        compiler_params=params(),
+        compiler_params=params(dimension_semantics=("arbitrary",)),
     )(ordered, g1, qkvt, owt, g2, w1t, w2t)
 
 
@@ -621,16 +630,13 @@
 ):
     feats_t = feats.T
     tap_t = tap_index.T
-    halo, fetch, own, away, spot, groups, blank, cwt, qkvt, owt, g1, g2, w1t = halo_exchange(
+    halo, fetch, own, away, spot, groups, cwt, qkvt, owt, g1, g2, w1t = halo_exchange(
         halo_rows[0], feats_t, hilbert_pos.reshape(32, 128), tap_t,
         conv_weight.reshape(TAPS * C, C), qkv_weight, out_weight,
         ln1_gain.reshape(1, C), ln2_gain.reshape(1, C), mlp_in,
     )
-    updated, source = conv(
-        groups, fetch.reshape(PTS), spot, tap_t, cwt, feats_t, halo,
-        blank.reshape(SLOTS),
-    )
-    ordered, spots = deal(updated, source.reshape(SLOTS // 128, 128))
+    updated = conv(groups, spot, tap_t, cwt, feats_t, halo)
+    ordered, spots = deal(updated, fetch)
     done = windows(ordered, g1, qkvt, owt, g2, w1t, mlp_out.T)
     kept, returned = back(done, spots, own)
     return collect(kept, returned, away).T

time: 160 us -> 153 us (0.956)
  Pallas kernels: 159 us -> 153 us
    pallas_call x2, Pallas kernels: 87.2 us -> 83.3 us  [the longest x1 60.4 us: windows(): pl.pallas_call(window_kernel, name='windows', grid=(PTS // WIN,), in_spec...]
    pallas_call x1, Pallas kernels: 27.8 us -> 25.6 us  [deal(): pl.pallas_call(deal_kernel, name='deal', in_specs=[VM, VM], out_specs=[VM...]
where the time goes in v5:
time: 153 us
  Pallas kernels  153 us (100%)
    pallas_call x1, Pallas kernels, windows(): pl.pallas_call(window_kernel, name='windows', grid=(PTS // WIN,), in_spec...  60.4 us
    pallas_call x1, Pallas kernels, deal(): pl.pallas_call(deal_kernel, name='deal', in_specs=[VM, VM], out_specs=[VM...  25.6 us
    pallas_call x1, Pallas kernels, conv(): pl.pallas_call(conv_kernel, name='conv', in_specs=[SM, VM, VM, ANY, ANY,...  22.9 us
    pallas_call x1, Pallas kernels, halo_exchange(): pl.pallas_call(halo_kernel, name='halo_exchange', in_specs=[VM, VM, VM, A...  21.5 us
    pallas_call x1, Pallas kernels, back(): pl.pallas_call(back_kernel, name='back', in_specs=[VM] * 3, out_specs=[VM...  16.4 us
    pallas_call x1, Pallas kernels, collect(): pl.pallas_call(collect_kernel, name='collect', grid=(PTS // WIDE,), in_sp...  6.23 us

profile of v5, /device:TPU:25, one launch (start us, length us, event | category | flops | bytes accessed | tf_op | source)
XLA Modules:
  0.0 153.0 jit_solution(17012345858527691921)
XLA Ops:
  0.0 21.5 %halo_exchange.1 = (bf16[8,192,512]{2,1,0:T(8,128)(2,1)}, s32[32,128]{1,0:T(8,128)}, s32[32,128]{1,0:T(8,128)}, s32[32,128]{1,0:T(8,128)}, s32[32,128]{1,0:T(8,1...) custom-call(s32[8,512]{1,0:T(8,128)} %bitcast.15, ...), custom_call_target="tpu_custom_call" | custom-call | tf_op jit(solution)/shard_map/halo_exchange/pallas_call | solution.py:232
  21.5 22.9 %conv.1.updated_ref = bf16[208,4096]{1,0:T(8,128)(2,1)} custom-call(s32[27,128]{1,0:T(8,128)} %get-tuple-element.21.group_ref, s32[32,128]{1,0:T(8,128)} %get-tuple-element.22.spot_ref, s32[27,4096]{1,0:T(8,128)} %bitcast.13, bf16[192,5184]{1,0:T(8,128)(2,1)} %get-tuple-element.23.cwt_ref, bf16[192,4096]{1,0:T(8,128)(2,1)} %bitcast.10, ...), custom_call_target="tpu_custom_call" | custom-call | tf_op jit(solution)/shard_map/conv/pallas_call | solution.py:322
  44.5 25.6 %deal.1 = (bf16[192,4096]{1,0:T(8,128)(2,1)}, s32[8,256]{1,0:T(8,128)}) custom-call(bf16[208,4096]{1,0:T(8,128)(2,1)} %conv.1.updated_ref, s32[32,128]{1,0:T(8,128)} %get-tuple-element.25.fetch_ref), custom_call_target="tpu_custom_call" | custom-call | tf_op jit(solution)/shard_map/deal/pallas_call | solution.py:423
  70.1 60.4 %windows.1.done_ref = bf16[192,4096]{1,0:T(8,128)(2,1)} custom-call(bf16[192,4096]{1,0:T(8,128)(2,1)} %get-tuple-element.26.in_ref, f32[192,128]{1,0:T(8,128)} %get-tuple-element.27.g1_ref, bf16[768,192]{1,0:T(8,128)(2,1)} %get-tuple-element.28.qkvt_ref, bf16[192,256]{1,0:T(8,128)(2,1)} %get-tuple-element.29.owt_ref, f32[192,128]{1,0:T(8,128)} %get-tuple-element.30.g2_ref, ...), custom_call_target="tpu_custom_call" | custom-call | tf_op jit(solution)/shard_map/windows/pallas_call | solution.py:507
  130.4 16.4 %back.1 = (bf16[192,4096]{1,0:T(8,128)(2,1)}, bf16[192,2048]{1,0:T(8,128)(2,1)}) custom-call(bf16[192,4096]{1,0:T(8,128)(2,1)} %windows.1.done_ref, s32[8,256]{1,0:T(8,128)} %get-tuple-element.32.spots_ref, s32[32,128]{1,0:T(8,128)} %get-tuple-element.33.own_ref), custom_call_target="tpu_custom_call" | custom-call | tf_op jit(solution)/shard_map/back/pallas_call | solution.py:578
  146.8 6.2 %collect.1 = bf16[192,4096]{1,0:T(8,128)(2,1)} custom-call(bf16[192,4096]{1,0:T(8,128)(2,1)} %get-tuple-element.34.kept_ref, bf16[192,2048]{1,0:T(8,128)(2,1)} %get-tuple-element.35.returned_ref, s32[32,128]{1,0:T(8,128)} %get-tuple-element.36.away_ref), custom_call_target="tpu_custom_call" | custom-call | tf_op jit(solution)/shard_map/collect/pallas_call | solution.py:611

commit v6 on v5

--- a/solution.py
+++ b/solution.py
@@ -193,17 +193,21 @@
         def _():
             pltpu.make_async_copy(zeros, out_ref.at[k], zero_sem.at[k]).start()
 
-    pl.semaphore_wait(barrier, count)
+    def fill(k):
+        select_columns(halo_ref[pl.ds(k, 1), :], onehot)
+        send[k] = jnp.dot(feats_ref[...], onehot[...], preferred_element_type=F32).astype(BF)
 
     def one(i, carry):
         pair = in_turn(i // 2)
         k = jnp.where(i % 2 == 0, pair, 7 - pair)
-        select_columns(halo_ref[pl.ds(k, 1), :], onehot)
-        send[k] = jnp.dot(feats_ref[...], onehot[...], preferred_element_type=F32).astype(BF)
+        fill(k)
         start(k)
         return carry
 
-    lax.fori_loop(0, 8, one, 0)
+    fill(0)
+    pl.semaphore_wait(barrier, count)
+    start(0)
+    lax.fori_loop(1, 8, one, 0)
     for load in loads:
         load.wait()
     prepare_weights(cw, qkvw, ow, g1_ref, g2_ref, w1, cwt, qkvt_ref, owt_ref, g1c_ref, g2c_ref, w1t_ref, pad)
@@ -361,22 +365,28 @@
 
     for r in range(PTS // 128):
         index[r * 128 : (r + 1) * 128, :] = spread_index(fetch_ref[r : r + 1, :])
-    pl.semaphore_wait(barrier, count)
     first = onehot_a.at[:, 0:CAP]
     second = onehot_b.at[:, 0:CAP]
 
+    def fill(k):
+        place_rows(index, PTS + k * CAP, first)
+        place_rows(index, PTS + (7 - k) * CAP, second)
+
+        send[k] = jnp.dot(updated_ref[...], first[...], preferred_element_type=F32).astype(BF)
+        send[7 - k] = jnp.dot(updated_ref[...], second[...], preferred_element_type=F32).astype(BF)
+
     def pair(i, carry):
         k = in_turn(i)
-        place_rows(index, PTS + k * CAP, first)
-        place_rows(index, PTS + (7 - k) * CAP, second)
-
-        send[k] = jnp.dot(updated_ref[...], first[...], preferred_element_type=F32).astype(BF)
-        send[7 - k] = jnp.dot(updated_ref[...], second[...], preferred_element_type=F32).astype(BF)
+        fill(k)
         start(k)
         start(7 - k)
         return carry
 
-    lax.fori_loop(0, 4, pair, 0)
+    fill(0)
+    pl.semaphore_wait(barrier, count)
+    start(0)
+    start(7)
+    lax.fori_loop(1, 4, pair, 0)
 
     def stay(m, carry):
         for n, onehot in ((2 * m, onehot_a), (2 * m + 1, onehot_b)):
@@ -537,22 +547,28 @@
         def _():
             push(k, send.at[k], landing(7 - k), send_sem, recv_sem).start()
 
-    pl.semaphore_wait(barrier, count)
     first = onehot_a.at[:, 0:CAP]
     second = onehot_b.at[:, 0:CAP]
 
+    def fill(k):
+        select_columns(spots_ref[pl.ds(k, 1), :], first)
+        select_columns(spots_ref[pl.ds(7 - k, 1), :], second)
+
+        send[k] = jnp.dot(done_ref[...], first[...], preferred_element_type=F32).astype(BF)
+        send[7 - k] = jnp.dot(done_ref[...], second[...], preferred_element_type=F32).astype(BF)
+
     def pair(i, carry):
         k = in_turn(i)
-        select_columns(spots_ref[pl.ds(k, 1), :], first)
-        select_columns(spots_ref[pl.ds(7 - k, 1), :], second)
-
-        send[k] = jnp.dot(done_ref[...], first[...], preferred_element_type=F32).astype(BF)
-        send[7 - k] = jnp.dot(done_ref[...], second[...], preferred_element_type=F32).astype(BF)
+        fill(k)
         start(k)
         start(7 - k)
         return carry
 
-    lax.fori_loop(0, 4, pair, 0)
+    fill(0)
+    pl.semaphore_wait(barrier, count)
+    start(0)
+    start(7)
+    lax.fori_loop(1, 4, pair, 0)
 
     def stay(m, carry):
         for n, onehot in ((2 * m, onehot_a), (2 * m + 1, onehot_b)):

time: 153 us -> 150 us (0.980)
  Pallas kernels: 153 us -> 150 us
    pallas_call x1, Pallas kernels: 25.6 us -> 23.9 us  [deal(): pl.pallas_call(deal_kernel, name='deal', in_specs=[VM, VM], out_specs=[VM...]
where the time goes in v6:
time: 150 us
  Pallas kernels  150 us (100%)
    pallas_call x1, Pallas kernels, windows(): pl.pallas_call(window_kernel, name='windows', grid=(PTS // WIN,), in_spec...  60.4 us
    pallas_call x1, Pallas kernels, deal(): pl.pallas_call(deal_kernel, name='deal', in_specs=[VM, VM], out_specs=[VM...  23.9 us
    pallas_call x1, Pallas kernels, conv(): pl.pallas_call(conv_kernel, name='conv', in_specs=[SM, VM, VM, ANY, ANY,...  22.9 us
    pallas_call x1, Pallas kernels, halo_exchange(): pl.pallas_call(halo_kernel, name='halo_exchange', in_specs=[VM, VM, VM, A...  21.2 us
    pallas_call x1, Pallas kernels, back(): pl.pallas_call(back_kernel, name='back', in_specs=[VM] * 3, out_specs=[VM...  15.3 us
    pallas_call x1, Pallas kernels, collect(): pl.pallas_call(collect_kernel, name='collect', grid=(PTS // WIDE,), in_sp...  6.22 us

profile of v6, /device:TPU:25, one launch (start us, length us, event | category | flops | bytes accessed | tf_op | source)
XLA Modules:
  0.0 149.9 jit_solution(28567278621594757)
XLA Ops:
  0.0 21.2 %halo_exchange.1 = (bf16[8,192,512]{2,1,0:T(8,128)(2,1)}, s32[32,128]{1,0:T(8,128)}, s32[32,128]{1,0:T(8,128)}, s32[32,128]{1,0:T(8,128)}, s32[32,128]{1,0:T(8,1...) custom-call(s32[8,512]{1,0:T(8,128)} %bitcast.15, ...), custom_call_target="tpu_custom_call" | custom-call | tf_op jit(solution)/shard_map/halo_exchange/pallas_call | solution.py:236
  21.2 22.9 %conv.1.updated_ref = bf16[208,4096]{1,0:T(8,128)(2,1)} custom-call(s32[27,128]{1,0:T(8,128)} %get-tuple-element.21.group_ref, s32[32,128]{1,0:T(8,128)} %get-tuple-element.22.spot_ref, s32[27,4096]{1,0:T(8,128)} %bitcast.13, bf16[192,5184]{1,0:T(8,128)(2,1)} %get-tuple-element.23.cwt_ref, bf16[192,4096]{1,0:T(8,128)(2,1)} %bitcast.10, ...), custom_call_target="tpu_custom_call" | custom-call | tf_op jit(solution)/shard_map/conv/pallas_call | solution.py:326
  44.0 23.9 %deal.1 = (bf16[192,4096]{1,0:T(8,128)(2,1)}, s32[8,256]{1,0:T(8,128)}) custom-call(bf16[208,4096]{1,0:T(8,128)(2,1)} %conv.1.updated_ref, s32[32,128]{1,0:T(8,128)} %get-tuple-element.25.fetch_ref), custom_call_target="tpu_custom_call" | custom-call | tf_op jit(solution)/shard_map/deal/pallas_call | solution.py:433
  67.9 60.4 %windows.1.done_ref = bf16[192,4096]{1,0:T(8,128)(2,1)} custom-call(bf16[192,4096]{1,0:T(8,128)(2,1)} %get-tuple-element.26.in_ref, f32[192,128]{1,0:T(8,128)} %get-tuple-element.27.g1_ref, bf16[768,192]{1,0:T(8,128)(2,1)} %get-tuple-element.28.qkvt_ref, bf16[192,256]{1,0:T(8,128)(2,1)} %get-tuple-element.29.owt_ref, f32[192,128]{1,0:T(8,128)} %get-tuple-element.30.g2_ref, ...), custom_call_target="tpu_custom_call" | custom-call | tf_op jit(solution)/shard_map/windows/pallas_call | solution.py:517
  128.3 15.3 %back.1 = (bf16[192,4096]{1,0:T(8,128)(2,1)}, bf16[192,2048]{1,0:T(8,128)(2,1)}) custom-call(bf16[192,4096]{1,0:T(8,128)(2,1)} %windows.1.done_ref, s32[8,256]{1,0:T(8,128)} %get-tuple-element.32.spots_ref, s32[32,128]{1,0:T(8,128)} %get-tuple-element.33.own_ref), custom_call_target="tpu_custom_call" | custom-call | tf_op jit(solution)/shard_map/back/pallas_call | solution.py:594
  143.6 6.2 %collect.1 = bf16[192,4096]{1,0:T(8,128)(2,1)} custom-call(bf16[192,4096]{1,0:T(8,128)(2,1)} %get-tuple-element.34.kept_ref, bf16[192,2048]{1,0:T(8,128)(2,1)} %get-tuple-element.35.returned_ref, s32[32,128]{1,0:T(8,128)} %get-tuple-element.36.away_ref), custom_call_target="tpu_custom_call" | custom-call | tf_op jit(solution)/shard_map/collect/pallas_call | solution.py:627

commit v7 on v6

--- a/solution.py
+++ b/solution.py
@@ -608,16 +608,15 @@
     )(done, spots, own)
 
 
-WIDE = 1024
+WIDE = 2048
 
 
 def collect_kernel(kept_ref, returned_ref, away_ref, out_ref, onehot_a, onehot_b):
     i = pl.program_id(0)
-    halves = ((0, onehot_a), (BLOCK, onehot_b))
-    for at, onehot in halves:
+    for at in range(0, WIDE, BLOCK):
+        onehot = (onehot_a, onehot_b)[at // BLOCK % 2]
         first = i * (WIDE // 128) + at // 128
         select_columns(index_row(away_ref, first, BLOCK // 128), onehot)
-    for at, onehot in halves:
         taken = jnp.dot(returned_ref[...], onehot[...], preferred_element_type=F32)
         kept = kept_ref[:, at : at + BLOCK].astype(F32)
         out_ref[:, at : at + BLOCK] = (kept + taken).astype(BF)

time: 150 us -> 150 us (level)
  no operation moved by 1% of the time
where the time goes in v7:
time: 150 us
  Pallas kernels  150 us (100%)
    pallas_call x1, Pallas kernels, windows(): pl.pallas_call(window_kernel, name='windows', grid=(PTS // WIN,), in_spec...  60.4 us
    pallas_call x1, Pallas kernels, deal(): pl.pallas_call(deal_kernel, name='deal', in_specs=[VM, VM], out_specs=[VM...  23.8 us
    pallas_call x1, Pallas kernels, conv(): pl.pallas_call(conv_kernel, name='conv', in_specs=[SM, VM, VM, ANY, ANY,...  22.9 us
    pallas_call x1, Pallas kernels, halo_exchange(): pl.pallas_call(halo_kernel, name='halo_exchange', in_specs=[VM, VM, VM, A...  21.2 us
    pallas_call x1, Pallas kernels, back(): pl.pallas_call(back_kernel, name='back', in_specs=[VM] * 3, out_specs=[VM...  15.3 us
    pallas_call x1, Pallas kernels, collect(): pl.pallas_call(collect_kernel, name='collect', grid=(PTS // WIDE,), in_sp...  5.95 us

profile of v7, /device:TPU:25, one launch (start us, length us, event | category | flops | bytes accessed | tf_op | source)
XLA Modules:
  0.0 149.6 jit_solution(918061260000705334)
XLA Ops:
  0.0 21.2 %halo_exchange.1 = (bf16[8,192,512]{2,1,0:T(8,128)(2,1)}, s32[32,128]{1,0:T(8,128)}, s32[32,128]{1,0:T(8,128)}, s32[32,128]{1,0:T(8,128)}, s32[32,128]{1,0:T(8,1...) custom-call(s32[8,512]{1,0:T(8,128)} %bitcast.15, ...), custom_call_target="tpu_custom_call" | custom-call | tf_op jit(solution)/shard_map/halo_exchange/pallas_call | solution.py:236
  21.2 22.9 %conv.1.updated_ref = bf16[208,4096]{1,0:T(8,128)(2,1)} custom-call(s32[27,128]{1,0:T(8,128)} %get-tuple-element.21.group_ref, s32[32,128]{1,0:T(8,128)} %get-tuple-element.22.spot_ref, s32[27,4096]{1,0:T(8,128)} %bitcast.13, bf16[192,5184]{1,0:T(8,128)(2,1)} %get-tuple-element.23.cwt_ref, bf16[192,4096]{1,0:T(8,128)(2,1)} %bitcast.10, ...), custom_call_target="tpu_custom_call" | custom-call | tf_op jit(solution)/shard_map/conv/pallas_call | solution.py:326
  44.1 23.8 %deal.1 = (bf16[192,4096]{1,0:T(8,128)(2,1)}, s32[8,256]{1,0:T(8,128)}) custom-call(bf16[208,4096]{1,0:T(8,128)(2,1)} %conv.1.updated_ref, s32[32,128]{1,0:T(8,128)} %get-tuple-element.25.fetch_ref), custom_call_target="tpu_custom_call" | custom-call | tf_op jit(solution)/shard_map/deal/pallas_call | solution.py:433
  67.9 60.4 %windows.1.done_ref = bf16[192,4096]{1,0:T(8,128)(2,1)} custom-call(bf16[192,4096]{1,0:T(8,128)(2,1)} %get-tuple-element.26.in_ref, f32[192,128]{1,0:T(8,128)} %get-tuple-element.27.g1_ref, bf16[768,192]{1,0:T(8,128)(2,1)} %get-tuple-element.28.qkvt_ref, bf16[192,256]{1,0:T(8,128)(2,1)} %get-tuple-element.29.owt_ref, f32[192,128]{1,0:T(8,128)} %get-tuple-element.30.g2_ref, ...), custom_call_target="tpu_custom_call" | custom-call | tf_op jit(solution)/shard_map/windows/pallas_call | solution.py:517
  128.3 15.3 %back.1 = (bf16[192,4096]{1,0:T(8,128)(2,1)}, bf16[192,2048]{1,0:T(8,128)(2,1)}) custom-call(bf16[192,4096]{1,0:T(8,128)(2,1)} %windows.1.done_ref, s32[8,256]{1,0:T(8,128)} %get-tuple-element.32.spots_ref, s32[32,128]{1,0:T(8,128)} %get-tuple-element.33.own_ref), custom_call_target="tpu_custom_call" | custom-call | tf_op jit(solution)/shard_map/back/pallas_call | solution.py:594
  143.7 5.9 %collect.1 = bf16[192,4096]{1,0:T(8,128)(2,1)} custom-call(bf16[192,4096]{1,0:T(8,128)(2,1)} %get-tuple-element.34.kept_ref, bf16[192,2048]{1,0:T(8,128)(2,1)} %get-tuple-element.35.returned_ref, s32[32,128]{1,0:T(8,128)} %get-tuple-element.36.away_ref), custom_call_target="tpu_custom_call" | custom-call | tf_op jit(solution)/shard_map/collect/pallas_call | solution.py:626
